TPU v7x, 512 devices: a whole 4x8x8 slice. The times are simulated.
512 devices in a mesh: sector: 256 (over z, y, x), chan: 2 (over core).
Axes of the slice: x: 4, y: 8, z: 8, core: 2. Of those that a mesh axis runs over, the one named last changes fastest.
Arguments:
- atm_state: bfloat16 [160, 262144], P('chan', 'sector'), may hold values from -6 to 6
- ocean_state: bfloat16 [160, 262144], P('chan', 'sector'), may hold values from -6 to 6
- wet_mask: int32 [262144], P('sector'), may hold values from 0 to 1, as said below
- neighbours: int32 [8, 262144], P(None, 'sector'), may hold values from 0 to 1087, as said below
- west_rim: int32 [8192], P('sector'), may hold values from 0 to 1023, as said below
- east_rim: int32 [8192], P('sector'), may hold values from 0 to 1023, as said below
- atm_gain: float32 [160], replicated, may hold values from 0.5 to 1.5
- atm_conv_in: bfloat16 [160, 9, 160], P('chan'), may hold values from -0.15625 to 0.15625
- atm_conv_out: bfloat16 [160, 9, 160], P('chan'), may hold values from -0.15625 to 0.15625
- ocean_conv: bfloat16 [160, 9, 160], P('chan'), may hold values from -0.15625 to 0.15625
- ocean_gain: float32 [160], replicated, may hold values from 0.5 to 1.5
- mlp_in: bfloat16 [640, 160], replicated, may hold values from -0.5 to 0.5
- mlp_out: bfloat16 [160, 640], replicated, may hold values from -0.25 to 0.25
Outputs:
- atm_next: bfloat16 [160, 262144], P('chan', 'sector')
- ocean_next: bfloat16 [160, 262144], P('chan', 'sector')
Inputs may be any that keep to these rules, and one draw needn't show every extreme that they name: Each sector is a grid of 32 cycles by 32 columns, stored cycle by cycle (32 positions to a cycle, cycle r at positions r * 32 to r * 32 + 31) with the columns in a permuted order within each cycle; a pixel's 8 neighbours are its compass neighbours on that grid, a cycle index beyond the grid's ends taken as the nearest cycle; a column beyond the west end refers to slot 1024 + cycle (the west sector's east rim pixel of that cycle), beyond the east end to slot 1056 + cycle. `west_rim`: the local positions of the sector's westmost column, cycle by cycle, consistent with neighbours. `east_rim`: the local positions of the sector's eastmost column, cycle by cycle, consistent with neighbours. `wet_mask`: the wet pixels of a sector and of the sector half the loop away number exactly 1024 together; some sector is all ocean.
All inputs are finite; a program needn't handle non-finite values.
Results may differ from a plain program's by a relative error of at most 0.013.
Values may be sent and summed in bfloat16 or wider, within the bound.
A program may use at most 64 MiB of HBM per device.

v0:
```python
import jax
import jax.numpy as jnp
from jax import lax
from jax.sharding import PartitionSpec as P

EPSILON = 1e-06


def padded_2(block, sides, width):
    for axis, dim in sides:
        count = lax.axis_size(axis)
        forward = [(i, i + 1) for i in range(count - 1)]
        forward.append((count - 1, 0))
        backward = [(target, source) for source, target in forward]
        low = lax.ppermute(
            lax.slice_in_dim(block, block.shape[dim] - width, None, axis=dim), axis, forward
        )
        high = lax.ppermute(lax.slice_in_dim(block, 0, width, axis=dim), axis, backward)
        block = jnp.concatenate([low, block, high], axis=dim)
    return block


def normalize(values_in, scales):
    values = values_in.astype(jnp.float32)
    mean_sq = jnp.mean(values * values, axis=0, keepdims=True)
    return (values * lax.rsqrt(mean_sq + EPSILON) * scales[:, None]).astype(jnp.bfloat16)


def gathered(values_in):
    return lax.all_gather(values_in, "chan", axis=0, tiled=True)


def with_rims(values_in, west_rim, east_rim):
    rim_rows = jnp.stack(
        [jnp.take(values_in, west_rim, axis=1), jnp.take(values_in, east_rim, axis=1)], axis=1
    )
    extended = padded_2(rim_rows, (("sector", 1),), 1)
    return jnp.concatenate([values_in, extended[:, 0], extended[:, 3]], axis=1)


def conv_input(values_in, scales, west_rim, east_rim):
    padded = with_rims(gathered(values_in), west_rim, east_rim)
    if scales is not None:
        padded = normalize(padded, scales)
    return padded


def stencil(padded, center_start, neighbours, weight, pixel_count):
    center = padded[:, center_start : center_start + pixel_count]
    running = jnp.dot(weight[:, 0, :], center, preferred_element_type=jnp.float32)
    for neighbour in range(8):
        moved = jnp.take(padded, neighbours[neighbour], axis=1)
        running = running + jnp.dot(
            weight[:, neighbour + 1, :], moved, preferred_element_type=jnp.float32
        )
    return running


def atmos_step(current, scales, w_first, w_second, neighbours, west_rim, east_rim):
    pixel_count = current.shape[1]
    padded = conv_input(current, scales, west_rim, east_rim)
    hidden = jax.nn.gelu(
        stencil(padded, 0, neighbours, w_first, pixel_count), approximate=True
    ).astype(jnp.bfloat16)
    padded_two = conv_input(hidden, None, west_rim, east_rim)
    return (
        current.astype(jnp.float32) + stencil(padded_two, 0, neighbours, w_second, pixel_count)
    ).astype(jnp.bfloat16)


def mix_columns(rows_in, scales, mlp_in, mlp_out):
    normed = normalize(rows_in, scales)
    hidden = jax.nn.gelu(
        jnp.dot(mlp_in, normed, preferred_element_type=jnp.float32), approximate=True
    ).astype(jnp.bfloat16)
    return jnp.dot(mlp_out, hidden, preferred_element_type=jnp.float32).astype(jnp.bfloat16)


def ocean_mix(row_block, scales, mlp_in, mlp_out):
    traded = lax.all_to_all(row_block, "chan", split_axis=1, concat_axis=0, tiled=True)
    update = mix_columns(traded, scales, mlp_in, mlp_out)
    return lax.all_to_all(update, "chan", split_axis=0, concat_axis=1, tiled=True)


def per_device(
    atm_state,
    ocean_state,
    wet_mask,
    neighbours,
    west_rim,
    east_rim,
    atm_gain,
    atm_conv_in,
    atm_conv_out,
    ocean_conv,
    ocean_gain,
    mlp_in,
    mlp_out,
):
    pixel_count = atm_state.shape[1]
    state_one = atmos_step(
        atm_state, atm_gain, atm_conv_in, atm_conv_out, neighbours, west_rim, east_rim
    )
    state_two = atmos_step(
        state_one, atm_gain, atm_conv_in, atm_conv_out, neighbours, west_rim, east_rim
    )
    wet_rows = wet_mask.astype(jnp.float32)[None, :]
    forcing = (
        (
            ocean_state.astype(jnp.float32)
            + 0.5 * (state_one.astype(jnp.float32) + state_two.astype(jnp.float32))
        )
        * wet_rows
    ).astype(jnp.bfloat16)
    padded = conv_input(forcing, None, west_rim, east_rim)
    mixed_rows = stencil(padded, 0, neighbours, ocean_conv, pixel_count).astype(jnp.bfloat16)
    update = ocean_mix(mixed_rows, ocean_gain, mlp_in, mlp_out)
    ocean_next = (ocean_state.astype(jnp.float32) + wet_rows * update.astype(jnp.float32)).astype(
        jnp.bfloat16
    )
    return (state_two, ocean_next)


def solution(mesh):
    in_specs = (
        P("chan", "sector"),
        P("chan", "sector"),
        P("sector"),
        P(None, "sector"),
        P("sector"),
        P("sector"),
        P(),
        P("chan", None, None),
        P("chan", None, None),
        P("chan", None, None),
        P(),
        P(),
        P(),
    )
    out_specs = (P("chan", "sector"), P("chan", "sector"))
    return jax.shard_map(
        per_device, mesh=mesh, in_specs=in_specs, out_specs=out_specs, check_vma=False
    )
```

profile of v0, /device:TPU:1, one launch (start us, length us, event | category | flops | bytes accessed | tf_op | source)
XLA Modules:
  0.0 332.1 jit_solution(7973424271023531104)
XLA Ops:
  2.0 8.8 %all_gather.15 = bf16[160,1024]{1,0:T(8,128)(2,1)S(1)} all-gather(bf16[80,1024]{1,0:T(8,128)(2,1)} %param.17), channel_id=1, replica_groups=mesh['sector'=256,'chan'=2] {'chan'}, dimensions={0}, use_global_device_ids=true | all-gather | bytes 491520 | tf_op jit(solution)/shard_map/all_gather | solution.py:30
  14.5 10.4 %collective-permute-start.1 = (bf16[160,1,32]{2,0,1:T(8,128)(2,1)S(1)}, bf16[160,1,32]{2,0,1:T(8,128)(2,1)S(1)}, u32[]{:S(2)}, u32[]{:S(2)}) collective-permute-start(bf16[160,1,32]{2,0,1:T(8,128)(2,1)S(1)} %select_bitcast_fusion.8), channel_id=1, source_target_pairs={{2,0},{4,2},{6,4},{8,6},{10,8},{12,10},{14,12},{16,14},{18,16},{20... | collective-permute-start | bytes 30728 | tf_op jit(solution)/shard_map/ppermute | solution.py:18
  27.0 5.0 %gather_fusion.2 = bf16[1024,160]{1,0:T(8,128)(2,1)} fusion(bf16[160,1088]{0,1:T(8,128)(2,1)S(1)} %copy.142, s32[1024]{0:T(1024)S(1)} %fusion.326), kind=kCustom, calls=%fused_computation.1.clone | custom fusion | bytes 659456 | tf_op jit(solution)/shard_map/jit(_take)/gather | solution.py:52
  32.0 4.9 %gather_fusion.3 = bf16[1024,160]{1,0:T(8,128)(2,1)} fusion(bf16[160,1088]{0,1:T(8,128)(2,1)S(1)} %copy.142, s32[1024]{0:T(1024)S(1)} %fusion.327), kind=kCustom, calls=%fused_computation.11.clone | custom fusion | bytes 659456 | tf_op jit(solution)/shard_map/jit(_take)/gather | solution.py:52
  36.9 4.9 %gather_fusion.4 = bf16[1024,160]{1,0:T(8,128)(2,1)} fusion(bf16[160,1088]{0,1:T(8,128)(2,1)S(1)} %copy.142, s32[1024]{0:T(1024)S(1)} %fusion.328), kind=kCustom, calls=%fused_computation.12.clone | custom fusion | bytes 659456 | tf_op jit(solution)/shard_map/jit(_take)/gather | solution.py:52
  45.8 3.9 %gather_fusion.6 = bf16[1024,160]{1,0:T(8,128)(2,1)S(1)} fusion(bf16[160,1088]{0,1:T(8,128)(2,1)S(1)} %copy.142, s32[1024]{0:T(1024)S(1)} %fusion.330), kind=kCustom, calls=%fused_computation.14.clone | custom fusion | bytes 659456 | tf_op jit(solution)/shard_map/jit(_take)/gather | solution.py:52
  49.8 3.9 %gather_fusion.7 = bf16[1024,160]{1,0:T(8,128)(2,1)S(1)} fusion(bf16[160,1088]{0,1:T(8,128)(2,1)S(1)} %copy.142, s32[1024]{0:T(1024)S(1)} %fusion.331), kind=kCustom, calls=%fused_computation.15.clone | custom fusion | bytes 659456 | tf_op jit(solution)/shard_map/jit(_take)/gather | solution.py:52
  53.7 3.9 %gather_fusion.8 = bf16[1024,160]{1,0:T(8,128)(2,1)S(1)} fusion(bf16[160,1088]{0,1:T(8,128)(2,1)S(1)} %copy.142, s32[1024]{0:T(1024)S(1)} %fusion.332), kind=kCustom, calls=%fused_computation.16.clone | custom fusion | bytes 659456 | tf_op jit(solution)/shard_map/jit(_take)/gather | solution.py:52
  57.7 5.0 %gather_fusion.9 = bf16[1024,160]{1,0:T(8,128)(2,1)} fusion(bf16[160,1088]{0,1:T(8,128)(2,1)S(1)} %copy.142, s32[1024]{0:T(1024)S(1)} %fusion.333), kind=kCustom, calls=%fused_computation.17.clone | custom fusion | bytes 659456 | tf_op jit(solution)/shard_map/jit(_take)/gather | solution.py:52
  73.1 9.4 %collective-permute-start.3 = (bf16[160,1,32]{2,0,1:T(8,128)(2,1)S(1)}, bf16[160,1,32]{2,0,1:T(8,128)(2,1)S(1)}, u32[]{:S(2)}, u32[]{:S(2)}) collective-permute-start(bf16[160,1,32]{2,0,1:T(8,128)(2,1)S(1)} %select_bitcast_fusion.6), channel_id=1, source_target_pairs={{2,0},{4,2},{6,4},{8,6},{10,8},{12,10},{14,12},{16,14},{18,16},{20... | collective-permute-start | bytes 30728 | tf_op jit(solution)/shard_map/ppermute | solution.py:18
  84.7 8.1 %collective-permute-done.2 = bf16[160,1,32]{2,0,1:T(8,128)(2,1)S(1)} collective-permute-done((bf16[160,1,32]{2,0,1:T(8,128)(2,1)S(1)}, bf16[160,1,32]{2,0,1:T(8,128)(2,1)S(1)}, u32[]{:S(2)}, u32[]{:S(2)}) %collective-permute-start.2) | collective-permute-done | bytes 10272 | tf_op jit(solution)/shard_map/ppermute | solution.py:15
  93.6 4.9 %gather_fusion.12 = bf16[1024,160]{1,0:T(8,128)(2,1)} fusion(bf16[160,1088]{0,1:T(8,128)(2,1)S(1)} %copy.154, s32[1024]{0:T(1024)S(1)} %copy-done.27), kind=kCustom, calls=%fused_computation.18.clone | custom fusion | bytes 659456 | tf_op jit(solution)/shard_map/jit(_take)/gather | solution.py:52
  98.5 4.9 %gather_fusion.13 = bf16[1024,160]{1,0:T(8,128)(2,1)} fusion(bf16[160,1088]{0,1:T(8,128)(2,1)S(1)} %copy.154, s32[1024]{0:T(1024)S(1)} %copy-done.32), kind=kCustom, calls=%fused_computation.19.clone | custom fusion | bytes 659456 | tf_op jit(solution)/shard_map/jit(_take)/gather | solution.py:52
  103.5 4.9 %gather_fusion.14 = bf16[1024,160]{1,0:T(8,128)(2,1)} fusion(bf16[160,1088]{0,1:T(8,128)(2,1)S(1)} %copy.154, s32[1024]{0:T(1024)S(1)} %copy-done.37), kind=kCustom, calls=%fused_computation.20.clone | custom fusion | bytes 659456 | tf_op jit(solution)/shard_map/jit(_take)/gather | solution.py:52
  112.4 3.9 %gather_fusion.16 = bf16[1024,160]{1,0:T(8,128)(2,1)S(1)} fusion(bf16[160,1088]{0,1:T(8,128)(2,1)S(1)} %copy.154, s32[1024]{0:T(1024)S(1)} %copy-done.47), kind=kCustom, calls=%fused_computation.22.clone | custom fusion | bytes 659456 | tf_op jit(solution)/shard_map/jit(_take)/gather | solution.py:52
  124.3 5.4 %gather_fusion.19 = bf16[1024,160]{1,0:T(8,128)(2,1)} fusion(bf16[160,1088]{0,1:T(8,128)(2,1)S(1)} %copy.154, s32[1024]{0:T(1024)} %copy-done.61), kind=kCustom, calls=%fused_computation.25.clone | custom fusion | bytes 659456 | tf_op jit(solution)/shard_map/jit(_take)/gather | solution.py:52
  147.7 6.6 %collective-permute-done.4 = bf16[160,1,32]{2,0,1:T(8,128)(2,1)S(1)} collective-permute-done((bf16[160,1,32]{2,0,1:T(8,128)(2,1)S(1)}, bf16[160,1,32]{2,0,1:T(8,128)(2,1)S(1)}, u32[]{:S(2)}, u32[]{:S(2)}) %collective-permute-start.4) | collective-permute-done | bytes 10272 | tf_op jit(solution)/shard_map/ppermute | solution.py:15
  155.8 4.9 %gather_fusion.22 = bf16[1024,160]{1,0:T(8,128)(2,1)} fusion(bf16[160,1088]{0,1:T(8,128)(2,1)S(1)} %copy.166, s32[1024]{0:T(1024)S(1)} %copy-done.28), kind=kCustom, calls=%fused_computation.26.clone | custom fusion | bytes 659456 | tf_op jit(solution)/shard_map/jit(_take)/gather | solution.py:52
  160.7 4.9 %gather_fusion.23 = bf16[1024,160]{1,0:T(8,128)(2,1)} fusion(bf16[160,1088]{0,1:T(8,128)(2,1)S(1)} %copy.166, s32[1024]{0:T(1024)S(1)} %copy-done.33), kind=kCustom, calls=%fused_computation.27.clone | custom fusion | bytes 659456 | tf_op jit(solution)/shard_map/jit(_take)/gather | solution.py:52
  165.7 4.9 %gather_fusion.24 = bf16[1024,160]{1,0:T(8,128)(2,1)} fusion(bf16[160,1088]{0,1:T(8,128)(2,1)S(1)} %copy.166, s32[1024]{0:T(1024)S(1)} %copy-done.38), kind=kCustom, calls=%fused_computation.28.clone | custom fusion | bytes 659456 | tf_op jit(solution)/shard_map/jit(_take)/gather | solution.py:52
  186.5 5.0 %gather_fusion.29 = bf16[1024,160]{1,0:T(8,128)(2,1)} fusion(bf16[160,1088]{0,1:T(8,128)(2,1)S(1)} %copy.166, s32[1024]{0:T(1024)S(1)} %copy-done.62), kind=kCustom, calls=%fused_computation.33.clone | custom fusion | bytes 659456 | tf_op jit(solution)/shard_map/jit(_take)/gather | solution.py:52
  208.8 5.9 %collective-permute-done.6 = bf16[160,1,32]{2,0,1:T(8,128)(2,1)S(1)} collective-permute-done((bf16[160,1,32]{2,0,1:T(8,128)(2,1)S(1)}, bf16[160,1,32]{2,0,1:T(8,128)(2,1)S(1)}, u32[]{:S(2)}, u32[]{:S(2)}) %collective-permute-start.6) | collective-permute-done | bytes 10272 | tf_op jit(solution)/shard_map/ppermute | solution.py:15
  215.5 4.9 %gather_fusion.32 = bf16[1024,160]{1,0:T(8,128)(2,1)} fusion(bf16[160,1088]{0,1:T(8,128)(2,1)S(1)} %copy.178, s32[1024]{0:T(1024)S(1)} %copy-done.29), kind=kCustom, calls=%fused_computation.34.clone | custom fusion | bytes 659456 | tf_op jit(solution)/shard_map/jit(_take)/gather | solution.py:52
  220.4 4.9 %gather_fusion.33 = bf16[1024,160]{1,0:T(8,128)(2,1)} fusion(bf16[160,1088]{0,1:T(8,128)(2,1)S(1)} %copy.178, s32[1024]{0:T(1024)S(1)} %copy-done.34), kind=kCustom, calls=%fused_computation.35.clone | custom fusion | bytes 659456 | tf_op jit(solution)/shard_map/jit(_take)/gather | solution.py:52
  225.4 4.9 %gather_fusion.34 = bf16[1024,160]{1,0:T(8,128)(2,1)} fusion(bf16[160,1088]{0,1:T(8,128)(2,1)S(1)} %copy.178, s32[1024]{0:T(1024)S(1)} %copy-done.39), kind=kCustom, calls=%fused_computation.36.clone | custom fusion | bytes 659456 | tf_op jit(solution)/shard_map/jit(_take)/gather | solution.py:52
  246.2 5.4 %gather_fusion.39 = bf16[1024,160]{1,0:T(8,128)(2,1)} fusion(bf16[160,1088]{0,1:T(8,128)(2,1)S(1)} %copy.178, s32[1024]{0:T(1024)} %copy-done.61), kind=kCustom, calls=%fused_computation.41.clone | custom fusion | bytes 659456 | tf_op jit(solution)/shard_map/jit(_take)/gather | solution.py:52
  270.1 6.5 %collective-permute-done.8 = bf16[160,1,32]{2,0,1:T(8,128)(2,1)S(1)} collective-permute-done((bf16[160,1,32]{2,0,1:T(8,128)(2,1)S(1)}, bf16[160,1,32]{2,0,1:T(8,128)(2,1)S(1)}, u32[]{:S(2)}, u32[]{:S(2)}) %collective-permute-start.8) | collective-permute-done | bytes 10272 | tf_op jit(solution)/shard_map/ppermute | solution.py:15
  277.4 4.9 %gather_fusion.42 = bf16[1024,160]{1,0:T(8,128)(2,1)} fusion(bf16[160,1088]{0,1:T(8,128)(2,1)S(1)} %copy.190, s32[1024]{0:T(1024)S(1)} %copy-done.30), kind=kCustom, calls=%fused_computation.42.clone | custom fusion | bytes 659456 | tf_op jit(solution)/shard_map/jit(_take)/gather | solution.py:52
  282.4 4.9 %gather_fusion.43 = bf16[1024,160]{1,0:T(8,128)(2,1)} fusion(bf16[160,1088]{0,1:T(8,128)(2,1)S(1)} %copy.190, s32[1024]{0:T(1024)S(1)} %copy-done.35), kind=kCustom, calls=%fused_computation.43.clone | custom fusion | bytes 659456 | tf_op jit(solution)/shard_map/jit(_take)/gather | solution.py:52
  287.3 5.0 %gather_fusion.44 = bf16[1024,160]{1,0:T(8,128)(2,1)} fusion(bf16[160,1088]{0,1:T(8,128)(2,1)S(1)} %copy.190, s32[1024]{0:T(1024)S(1)} %copy-done.40), kind=kCustom, calls=%fused_computation.44.clone | custom fusion | bytes 659456 | tf_op jit(solution)/shard_map/jit(_take)/gather | solution.py:52
  308.1 5.4 %gather_fusion.49 = bf16[1024,160]{1,0:T(8,128)(2,1)} fusion(bf16[160,1088]{0,1:T(8,128)(2,1)S(1)} %copy.190, s32[1024]{0:T(1024)} %copy-done.61), kind=kCustom, calls=%fused_computation.49.clone | custom fusion | bytes 659456 | tf_op jit(solution)/shard_map/jit(_take)/gather | solution.py:52
  320.5 5.1 %all_to_all.26 = bf16[80,2,512]{2,0,1:T(8,128)(2,1)S(1)} all-to-all(bf16[80,2,512]{2,0,1:T(8,128)(2,1)S(1)} %bitcast.368), channel_id=1, replica_groups=mesh['sector'=256,'chan'=2] {'chan'}, dimensions={1} | all-to-all | bytes 327680 | tf_op jit(solution)/shard_map/all_to_all | solution.py:80
  (383 shorter events, 153.2 us)
Async XLA Ops:
  0.6 325.2 %copy-start = (bf16[160,640]{1,0:T(8,128)(2,1)S(1)}, bf16[160,640]{1,0:T(8,128)(2,1)}, u32[]{:S(2)}) copy-start(bf16[160,640]{1,0:T(8,128)(2,1)} %param.29) | copy-start | bytes 614404
  2.0 80.6 %copy-start.86 = (pred[32]{0:T(512)(128)(4,1)}, pred[32]{0:T(512)(128)(4,1)S(1)}, u32[]{:S(2)}) copy-start(pred[32]{0:T(512)(128)(4,1)S(1)} %compare_and_fusion.9) | copy-start | bytes 100
  2.0 70.3 %copy-start.92 = (s32[1024]{0:T(1024)}, s32[1024]{0:T(1024)S(1)}, u32[]{:S(2)}) copy-start(s32[1024]{0:T(1024)S(1)} %pad_clamp_fusion.1) | copy-start | bytes 12292
  11.0 13.9 %copy-start.83 = (s32[8,1024]{1,0:T(8,128)S(1)}, s32[8,1024]{1,0:T(8,128)}, u32[]{:S(2)}) copy-start(s32[8,1024]{1,0:T(8,128)} %param.20) | copy-start | bytes 98308
  11.8 13.6 %collective-permute-start = (bf16[160,1,32]{2,0,1:T(8,128)(2,1)S(1)}, bf16[160,1,32]{2,0,1:T(8,128)(2,1)S(1)}, u32[]{:S(2)}, u32[]{:S(2)}) collective-permute-start(bf16[160,1,32]{2,0,1:T(8,128)(2,1)S(1)} %select_bitcast_fusion.9), channel_id=1, source_target_pairs={{0,2},{2,4},{4,6},{6,8},{8,10},{10,12},{12,14},{14,16},{16,18},{18... | collective-permute-start | bytes 30728 | tf_op jit(solution)/shard_map/ppermute | solution.py:15
  13.7 59.3 %copy-start.89 = (pred[32]{0:T(512)(128)(4,1)}, pred[32]{0:T(512)(128)(4,1)S(1)}, u32[]{:S(2)}) copy-start(pred[32]{0:T(512)(128)(4,1)S(1)} %compare_and_fusion.8) | copy-start | bytes 100
  13.8 57.9 %copy-start.93 = (s32[1024]{0:T(1024)}, s32[1024]{0:T(1024)S(1)}, u32[]{:S(2)}) copy-start(s32[1024]{0:T(1024)S(1)} %pad_clamp_fusion) | copy-start | bytes 12292
  14.5 11.5 %collective-permute-start.1 = (bf16[160,1,32]{2,0,1:T(8,128)(2,1)S(1)}, bf16[160,1,32]{2,0,1:T(8,128)(2,1)S(1)}, u32[]{:S(2)}, u32[]{:S(2)}) collective-permute-start(bf16[160,1,32]{2,0,1:T(8,128)(2,1)S(1)} %select_bitcast_fusion.8), channel_id=1, source_target_pairs={{2,0},{4,2},{6,4},{8,6},{10,8},{12,10},{14,12},{16,14},{18,16},{20... | collective-permute-start | bytes 30728 | tf_op jit(solution)/shard_map/ppermute | solution.py:18
  25.0 37.7 %copy-start.102 = (pred[1024]{0:T(1024)(128)(4,1)}, pred[1024]{0:T(1024)(128)(4,1)S(1)}, u32[]{:S(2)}) copy-start(pred[1024]{0:T(1024)(128)(4,1)S(1)} %compare_and_fusion.7) | copy-start | bytes 3076
  25.0 7.0 %copy-start.31 = (s32[1024]{0:T(1024)}, s32[1024]{0:T(1024)S(1)}, u32[]{:S(2)}) copy-start(s32[1024]{0:T(1024)S(1)} %fusion.327) | copy-start | bytes 12292
  25.1 39.1 %copy-start.104 = (pred[1024]{0:T(1024)(128)(4,1)}, pred[1024]{0:T(1024)(128)(4,1)S(1)}, u32[]{:S(2)}) copy-start(pred[1024]{0:T(1024)(128)(4,1)S(1)} %compare_and_fusion.6) | copy-start | bytes 3076
  25.1 11.9 %copy-start.36 = (s32[1024]{0:T(1024)}, s32[1024]{0:T(1024)S(1)}, u32[]{:S(2)}) copy-start(s32[1024]{0:T(1024)S(1)} %fusion.328) | copy-start | bytes 12292
  25.1 39.7 %copy-start.79 = (pred[1024]{0:T(1024)(128)(4,1)}, pred[1024]{0:T(1024)(128)(4,1)S(1)}, u32[]{:S(2)}) copy-start(pred[1024]{0:T(1024)(128)(4,1)S(1)} %compare_and_fusion.5) | copy-start | bytes 3076
  25.1 16.8 %copy-start.41 = (s32[1024]{0:T(1024)}, s32[1024]{0:T(1024)S(1)}, u32[]{:S(2)}) copy-start(s32[1024]{0:T(1024)S(1)} %fusion.329) | copy-start | bytes 12292
  25.1 40.8 %copy-start.75 = (pred[1024]{0:T(1024)(128)(4,1)}, pred[1024]{0:T(1024)(128)(4,1)S(1)}, u32[]{:S(2)}) copy-start(pred[1024]{0:T(1024)(128)(4,1)S(1)} %compare_and_fusion.4) | copy-start | bytes 3076
  25.2 20.6 %copy-start.46 = (s32[1024]{0:T(1024)}, s32[1024]{0:T(1024)S(1)}, u32[]{:S(2)}) copy-start(s32[1024]{0:T(1024)S(1)} %fusion.330) | copy-start | bytes 12292
  25.2 41.2 %copy-start.71 = (pred[1024]{0:T(1024)(128)(4,1)}, pred[1024]{0:T(1024)(128)(4,1)S(1)}, u32[]{:S(2)}) copy-start(pred[1024]{0:T(1024)(128)(4,1)S(1)} %compare_and_fusion.3) | copy-start | bytes 3076
  25.2 24.6 %copy-start.51 = (s32[1024]{0:T(1024)}, s32[1024]{0:T(1024)S(1)}, u32[]{:S(2)}) copy-start(s32[1024]{0:T(1024)S(1)} %fusion.331) | copy-start | bytes 12292
  25.2 41.5 %copy-start.67 = (pred[1024]{0:T(1024)(128)(4,1)}, pred[1024]{0:T(1024)(128)(4,1)S(1)}, u32[]{:S(2)}) copy-start(pred[1024]{0:T(1024)(128)(4,1)S(1)} %compare_and_fusion.2) | copy-start | bytes 3076
  25.3 28.5 %copy-start.56 = (s32[1024]{0:T(1024)}, s32[1024]{0:T(1024)S(1)}, u32[]{:S(2)}) copy-start(s32[1024]{0:T(1024)S(1)} %fusion.332) | copy-start | bytes 12292
  25.3 41.8 %copy-start.63 = (pred[1024]{0:T(1024)(128)(4,1)}, pred[1024]{0:T(1024)(128)(4,1)S(1)}, u32[]{:S(2)}) copy-start(pred[1024]{0:T(1024)(128)(4,1)S(1)} %compare_and_fusion.1) | copy-start | bytes 3076
  25.3 32.4 %copy-start.61 = (s32[1024]{0:T(1024)}, s32[1024]{0:T(1024)S(1)}, u32[]{:S(2)}) copy-start(s32[1024]{0:T(1024)S(1)} %fusion.333) | copy-start | bytes 12292
  25.3 42.1 %copy-start.98 = (pred[1024]{0:T(1024)(128)(4,1)}, pred[1024]{0:T(1024)(128)(4,1)S(1)}, u32[]{:S(2)}) copy-start(pred[1024]{0:T(1024)(128)(4,1)S(1)} %compare_and_fusion) | copy-start | bytes 3076
  73.1 11.6 %collective-permute-start.3 = (bf16[160,1,32]{2,0,1:T(8,128)(2,1)S(1)}, bf16[160,1,32]{2,0,1:T(8,128)(2,1)S(1)}, u32[]{:S(2)}, u32[]{:S(2)}) collective-permute-start(bf16[160,1,32]{2,0,1:T(8,128)(2,1)S(1)} %select_bitcast_fusion.6), channel_id=1, source_target_pairs={{2,0},{4,2},{6,4},{8,6},{10,8},{12,10},{14,12},{16,14},{18,16},{20... | collective-permute-start | bytes 30728 | tf_op jit(solution)/shard_map/ppermute | solution.py:18
  82.6 10.2 %collective-permute-start.2 = (bf16[160,1,32]{2,0,1:T(8,128)(2,1)S(1)}, bf16[160,1,32]{2,0,1:T(8,128)(2,1)S(1)}, u32[]{:S(2)}, u32[]{:S(2)}) collective-permute-start(bf16[160,1,32]{2,0,1:T(8,128)(2,1)S(1)} %select_bitcast_fusion.7), channel_id=1, source_target_pairs={{0,2},{2,4},{4,6},{6,8},{8,10},{10,12},{12,14},{14,16},{16,18},{18... | collective-permute-start | bytes 30728 | tf_op jit(solution)/shard_map/ppermute | solution.py:15
  142.0 5.7 %collective-permute-start.5 = (bf16[160,1,32]{2,0,1:T(8,128)(2,1)S(1)}, bf16[160,1,32]{2,0,1:T(8,128)(2,1)S(1)}, u32[]{:S(2)}, u32[]{:S(2)}) collective-permute-start(bf16[160,1,32]{2,0,1:T(8,128)(2,1)S(1)} %select_bitcast_fusion.4), channel_id=1, source_target_pairs={{2,0},{4,2},{6,4},{8,6},{10,8},{12,10},{14,12},{16,14},{18,16},{20... | collective-permute-start | bytes 30728 | tf_op jit(solution)/shard_map/ppermute | solution.py:18
  144.1 10.2 %collective-permute-start.4 = (bf16[160,1,32]{2,0,1:T(8,128)(2,1)S(1)}, bf16[160,1,32]{2,0,1:T(8,128)(2,1)S(1)}, u32[]{:S(2)}, u32[]{:S(2)}) collective-permute-start(bf16[160,1,32]{2,0,1:T(8,128)(2,1)S(1)} %select_bitcast_fusion.5), channel_id=1, source_target_pairs={{0,2},{2,4},{4,6},{6,8},{8,10},{10,12},{12,14},{14,16},{16,18},{18... | collective-permute-start | bytes 30728 | tf_op jit(solution)/shard_map/ppermute | solution.py:15
  200.7 7.5 %copy-start.96 = (s32[1024]{0:T(1024)S(1)}, s32[1024]{0:T(1024)}, u32[]{:S(2)}) copy-start(s32[1024]{0:T(1024)} %param.19) | copy-start | bytes 12292
  202.5 6.3 %collective-permute-start.7 = (bf16[160,1,32]{2,0,1:T(8,128)(2,1)S(1)}, bf16[160,1,32]{2,0,1:T(8,128)(2,1)S(1)}, u32[]{:S(2)}, u32[]{:S(2)}) collective-permute-start(bf16[160,1,32]{2,0,1:T(8,128)(2,1)S(1)} %select_bitcast_fusion.2), channel_id=1, source_target_pairs={{2,0},{4,2},{6,4},{8,6},{10,8},{12,10},{14,12},{16,14},{18,16},{20... | collective-permute-start | bytes 30728 | tf_op jit(solution)/shard_map/ppermute | solution.py:18
  204.5 10.2 %collective-permute-start.6 = (bf16[160,1,32]{2,0,1:T(8,128)(2,1)S(1)}, bf16[160,1,32]{2,0,1:T(8,128)(2,1)S(1)}, u32[]{:S(2)}, u32[]{:S(2)}) collective-permute-start(bf16[160,1,32]{2,0,1:T(8,128)(2,1)S(1)} %select_bitcast_fusion.3), channel_id=1, source_target_pairs={{0,2},{2,4},{4,6},{6,8},{8,10},{10,12},{12,14},{14,16},{16,18},{18... | collective-permute-start | bytes 30728 | tf_op jit(solution)/shard_map/ppermute | solution.py:15
  264.4 5.7 %collective-permute-start.9 = (bf16[160,1,32]{2,0,1:T(8,128)(2,1)S(1)}, bf16[160,1,32]{2,0,1:T(8,128)(2,1)S(1)}, u32[]{:S(2)}, u32[]{:S(2)}) collective-permute-start(bf16[160,1,32]{2,0,1:T(8,128)(2,1)S(1)} %select_bitcast_fusion), channel_id=1, source_target_pairs={{2,0},{4,2},{6,4},{8,6},{10,8},{12,10},{14,12},{16,14},{18,16},{20... | collective-permute-start | bytes 30728 | tf_op jit(solution)/shard_map/ppermute | solution.py:18
  266.5 10.2 %collective-permute-start.8 = (bf16[160,1,32]{2,0,1:T(8,128)(2,1)S(1)}, bf16[160,1,32]{2,0,1:T(8,128)(2,1)S(1)}, u32[]{:S(2)}, u32[]{:S(2)}) collective-permute-start(bf16[160,1,32]{2,0,1:T(8,128)(2,1)S(1)} %select_bitcast_fusion.1), channel_id=1, source_target_pairs={{0,2},{2,4},{4,6},{6,8},{8,10},{10,12},{12,14},{14,16},{16,18},{18... | collective-permute-start | bytes 30728 | tf_op jit(solution)/shard_map/ppermute | solution.py:15
  (88 other events, 211.9 us)
where the time goes:
time: 334 us; the launch traced here: 332 us
  local copies, waits for them, and re-layouts  205 us (61%)
  starting transfers between devices  40.4 us (12%)
  blocking collectives  30.5 us (9%)
  waiting for transfers between devices  27.7 us (8%)
  matrix products  22.7 us (7%)
  other arithmetic  3.5 us (1%)
    gather x40, local copies, waits for them, and re-layouts, stencil(): moved = jnp.take(padded, neighbours[neighbour], axis=1)  179 us
    ppermute x5, waiting for transfers between devices, padded_2(): lax.ppermute(lax.slice_in_dim(block, block.shape[dim] - width, None, axis...  27.1 us
    ppermute x5, starting transfers between devices, padded_2(): lax.ppermute(lax.slice_in_dim(block, 0, width, axis=dim), axis, backward)  25.5 us
    all_gather x5, blocking collectives, gathered(): return lax.all_gather(values_in, 'chan', axis=0, tiled=True)  21.5 us
    dot_general x40, matrix products, stencil(): jnp.dot(weight[:, neighbour + 1, :], moved, preferred_element_type=jnp.fl...  20.9 us
    unnamed x220, local copies, waits for them, and re-layouts  15 us
    ppermute x5, starting transfers between devices, padded_2(): lax.ppermute(lax.slice_in_dim(block, block.shape[dim] - width, None, axis...  14.9 us
  transfers between devices with their start and end apart: 10, of which 5 were waited for; matrix products, arithmetic and copies ran while one was open for 1% of the time, Pallas kernels for 0%

commit v1 on v0

v1 whole, which is shorter than its diff:
```python
import functools

import jax
import jax.numpy as jnp
from jax import lax
from jax.experimental import pallas as pl
from jax.experimental.pallas import tpu as pltpu
from jax.sharding import PartitionSpec as P

EPSILON = 1e-06
CH = 80
C = 160
ROWS = 32
STRIDE = 48
BUF = 1104
MESH = pl.DeviceIdType.MESH
NT = (((1,), (1,)), ((), ()))
TN = (((0,), (0,)), ((), ()))
F32 = jnp.float32
BF = jnp.bfloat16


def iota(shape, dim):
    return lax.broadcasted_iota(jnp.int32, shape, dim)


def onehot(hit):
    return jnp.where(hit, 1.0, 0.0).astype(BF)


def tap_slot(dyi, dxi):
    m = 3 * dyi + dxi
    return 0 if m == 4 else (m + 1 if m < 4 else m)


def kernel(
    nb, wet, ga, go, atm, oc, w1, w2, w3, mi, mo,
    out_a, out_o,
    xa, xo, wraw, wb, miv, mov, keys, tsel, sbuf, halo, st_a, st_b, oc_a, oc_b,
    va, vb, bc, pbuf, nrm, fin, obuf, nbv,
    lsem, psem_s, psem_r, hsem_s, hsem_r, osem_s, osem_r,
):
    sectors = lax.axis_size("sector")
    s = lax.axis_index("sector")
    c = lax.axis_index("chan")
    pc = 1 - c
    west = lax.rem(s + sectors - 1, sectors)
    east = lax.rem(s + 1, sectors)
    partner = {"sector": s, "chan": pc}

    bar = pltpu.get_barrier_semaphore()
    pl.semaphore_signal(bar, inc=1, device_id=partner, device_id_type=MESH)
    for chip in (west, east):
        for t in range(2):
            pl.semaphore_signal(
                bar, inc=1, device_id={"sector": chip, "chan": t}, device_id_type=MESH
            )

    loads = [
        pltpu.make_async_copy(nb, nbv, lsem.at[0]),
        pltpu.make_async_copy(atm, xa.at[c], lsem.at[1]),
        pltpu.make_async_copy(oc, xo.at[c], lsem.at[2]),
        pltpu.make_async_copy(w1, wraw.at[0, c], lsem.at[3]),
        pltpu.make_async_copy(w2, wraw.at[1, c], lsem.at[4]),
        pltpu.make_async_copy(w3, wraw.at[2, c], lsem.at[5]),
        pltpu.make_async_copy(mi, miv, lsem.at[6]),
        pltpu.make_async_copy(mo, mov, lsem.at[7]),
    ]
    for load in loads:
        load.start()
    loads[0].wait()

    for b in range(8):
        lane = iota((8, 128), 1)
        v = jnp.broadcast_to(nbv[3:4, 128 * b : 128 * b + 128], (8, 128))
        inside = v < 1024
        hop = jnp.where(inside, v - 128 * b, lane)
        col = jnp.where(inside, 1, 0)
        for _ in range(5):
            col = col + jnp.take_along_axis(col, hop, axis=1, mode="promise_in_bounds")
            hop = jnp.take_along_axis(hop, hop, axis=1, mode="promise_in_bounds")
        cyc = 4 * b + lax.shift_right_logical(lane, 5)
        keys[0, :, 128 * b : 128 * b + 128] = 32 * cyc + col
        keys[1, :, 128 * b : 128 * b + 128] = 32 * (31 - cyc) + col

    loads[1].wait()
    loads[2].wait()

    wet16 = jnp.broadcast_to(wet[...], (16, 1024)).astype(F32).astype(BF)

    hr = iota((256, 256), 0)
    hh = hr & 127
    far = hr >= 128
    hi = lax.shift_right_logical(hh * 205, 10)
    he = hh - 5 * hi
    key_a = jnp.where(hh < 105, 32 * hi + jnp.where(far, 27 + he, he), -1)
    key_o = jnp.where(
        (hh >= 105) & (hh < 122), 32 * (hh - 105) + jnp.where(far, 31, 0), -1
    )
    z16 = jnp.zeros((16, 256), BF)
    for t in range(2):
        total = jnp.zeros((96, 256), F32)
        for b in range(3):
            q = 256 * (b if t == 0 else 3 - b)
            key_q = keys[t, 0:1, q : q + 256]
            x_a = jnp.concatenate([xa[c, :, q : q + 256], z16], axis=0)
            x_o = jnp.concatenate([xo[c, :, q : q + 256], wet16[:, q : q + 256]], axis=0)
            total = total + lax.dot_general(
                x_a, onehot(key_a == key_q), NT, preferred_element_type=F32
            )
            total = total + lax.dot_general(
                x_o, onehot(key_o == key_q), NT, preferred_element_type=F32
            )
        sbuf[t, 0] = total[:, :128].astype(BF)
        sbuf[t, 1] = total[:, 128:].astype(BF)

    pl.semaphore_wait(bar, 5)

    halo_copies = []
    for t in range(2):
        for d, chip in ((0, west), (1, east)):
            halo_copies.append(
                pltpu.make_async_remote_copy(
                    src_ref=sbuf.at[t, d],
                    dst_ref=halo.at[c, :, pl.ds(128 * d, 128)],
                    send_sem=hsem_s.at[2 * t + d],
                    recv_sem=hsem_r.at[d, c],
                    device_id={"sector": chip, "chan": t},
                    device_id_type=MESH,
                )
            )
    for copy in halo_copies:
        copy.start()

    def to_partner(src, dst, n):
        return pltpu.make_async_remote_copy(
            src_ref=src,
            dst_ref=dst,
            send_sem=psem_s.at[n],
            recv_sem=psem_r.at[n],
            device_id=partner,
            device_id_type=MESH,
        )

    window = pl.ds(pl.multiple_of(256 * pc, 256), 768)
    pair = [
        to_partner(atm.at[:, window], xa.at[c, :, window], 0),
        to_partner(w1, wraw.at[0, c], 1),
        to_partner(oc.at[:, window], xo.at[c, :, window], 2),
        to_partner(w2, wraw.at[1, c], 3),
        to_partner(w3, wraw.at[2, c], 4),
    ]
    for copy in pair:
        copy.start()

    for b in range(3):
        q = pl.multiple_of(256 * jnp.where(c == 0, b, 3 - b), 256)
        key_q = keys[c, 0:1, pl.ds(q, 256)] - 256 * b
        tsel[b] = onehot(iota((256, 256), 0) == key_q)

    def prepare(n):
        wb[n, :, 480:512] = jnp.zeros((512, 32), BF)
        wb[n, 480:512, :] = jnp.zeros((32, 512), BF)
        for dyi in range(3):
            for dxi in range(3):
                k = jnp.where(c == 0, tap_slot(dyi, dxi), tap_slot(2 - dyi, dxi))
                w_0 = wraw[n, 0, k]
                w_1 = wraw[n, 1, k]
                for lanes, dst, width in (
                    (slice(0, 128), 128 * dyi, 128),
                    (slice(128, 160), 384 + 32 * dyi, 32),
                ):
                    r = 128 * dxi
                    wb[n, r : r + 80, dst : dst + width] = w_0[:, lanes]
                    wb[n, r + 80 : r + 128, dst : dst + width] = w_1[0:48, lanes]
                    r = 384 + 32 * dxi
                    wb[n, r : r + 32, dst : dst + width] = w_1[48:80, lanes]

    loads[3].wait()
    pair[1].wait_recv()
    prepare(0)

    gain_a = ga[:, 0:128]
    gain_b = jnp.concatenate([ga[:, 128:160], jnp.zeros((1, 96), F32)], axis=1)
    ocean_a = go[:, 0:128]
    ocean_b = jnp.concatenate([go[:, 128:160], jnp.zeros((1, 96), F32)], axis=1)

    pair[0].wait_recv()
    pair[2].wait_recv()
    for b in range(3):
        q = pl.multiple_of(256 * jnp.where(c == 0, b, 3 - b), 256)
        x_a = jnp.concatenate(
            [xa[0, :, pl.ds(q, 256)], xa[1, :, pl.ds(q, 256)], jnp.zeros((96, 256), BF)], axis=0
        )
        wet_b = jnp.broadcast_to(wet[:, pl.ds(q, 256)], (16, 256)).astype(F32).astype(BF)
        x_o = jnp.concatenate(
            [xo[0, :, pl.ds(q, 256)], xo[1, :, pl.ds(q, 256)], wet_b, jnp.zeros((80, 256), BF)],
            axis=0,
        )
        v_a = lax.dot_general(tsel[b], x_a, NT, preferred_element_type=F32)
        v_o = lax.dot_general(tsel[b], x_o, NT, preferred_element_type=F32)
        for il in range(8):
            i = 8 * b + il
            rows = slice(32 * il, 32 * il + 32)
            for g in [STRIDE * (i + 1) + 16] + ([16] if i == 0 else []):
                if i <= 20:
                    st_a[g : g + 32] = v_a[rows, :128]
                    st_b[g : g + 32] = v_a[rows, 128:]
                if i <= 16:
                    oc_a[g : g + 32] = v_o[rows, :128]
                    oc_b[g : g + 32] = v_o[rows, 128:]

    for d in range(2):
        for sender in range(2):
            pltpu.make_async_remote_copy(
                src_ref=sbuf.at[0, d],
                dst_ref=halo.at[sender, :, pl.ds(128 * d, 128)],
                send_sem=hsem_s.at[0],
                recv_sem=hsem_r.at[d, sender],
                device_id=partner,
                device_id_type=MESH,
            ).wait_recv()
    h_all = jnp.concatenate(
        [halo[0, 0:80], halo[1, 0:80], halo[0, 80:96], jnp.zeros((80, 256), BF)], axis=0
    )
    hl = iota((1, 256), 1)
    hh = hl & 127
    far = hl >= 128
    hi = lax.shift_right_logical(hh * 205, 10)
    he = hh - 5 * hi
    p1 = jnp.where(hh < 105, jnp.where(far, 16 * hi + 27 + he, 16 * hi + 32 + he), -1)
    p2 = jnp.where(hi == 0, p1 - 16, p1)
    r = iota((368, 256), 0)
    v_a = lax.dot_general(
        onehot((r == p1) | (r == p2)), h_all, NT, preferred_element_type=F32
    )
    oi = hh - 105
    p1 = jnp.where(
        (oi >= 0) & (oi < 17), jnp.where(far, 16 * oi + 31, 16 * oi + 32), -1
    )
    p2 = jnp.where(oi == 0, p1 - 16, p1)
    r = iota((304, 256), 0)
    v_o = lax.dot_general(
        onehot((r == p1) | (r == p2)), h_all, NT, preferred_element_type=F32
    )
    for k in range(23):
        rows = slice(16 * k, 16 * k + 16)
        g = STRIDE * k
        st_a[g : g + 16] = v_a[rows, :128]
        st_b[g : g + 16] = v_a[rows, 128:]
        if k < 19:
            oc_a[g : g + 16] = v_o[rows, :128]
            oc_b[g : g + 16] = v_o[rows, 128:]

    low = iota((STRIDE, 128), 1) < 32

    def normed(x_a, x_b, scale_a, scale_b):
        x_b = jnp.where(low, x_b, 0.0)
        mean_sq = jnp.sum(x_a * x_a + x_b * x_b, axis=1, keepdims=True) * (1.0 / C)
        inv = lax.rsqrt(mean_sq + EPSILON)
        return x_a * inv * scale_a, x_b * inv * scale_b

    def put(g, x_a, x_b):
        va[pl.ds(g, STRIDE)] = x_a.astype(BF)
        vb[pl.ds(g, STRIDE)] = jnp.where(low, x_b, 0.0).astype(BF).astype(F32)

    @pl.loop(0, 22)
    def _(m):
        g = pl.multiple_of(STRIDE * m, STRIDE)
        x_a, x_b = normed(
            st_a[pl.ds(g, STRIDE)], st_b[pl.ds(g, STRIDE)], gain_a, gain_b
        )
        put(g, x_a, x_b)

    top = slice(1056, 1072)
    x_a, x_b = st_a[top], st_b[top]
    mean_sq = jnp.sum(x_a * x_a + x_b * x_b, axis=1, keepdims=True) * (1.0 / C)
    inv = lax.rsqrt(mean_sq + EPSILON)
    va[top] = (x_a * inv * gain_a).astype(BF)
    vb[top] = (x_b * inv * gain_b).astype(BF).astype(F32)

    def convolve(n, wi, epilogue):
        size = 16 + STRIDE * n

        @pl.loop(0, n + 1)
        def _(m):
            g = pl.multiple_of(STRIDE * m + STRIDE, STRIDE)
            bc[pl.ds(g, STRIDE)] = (
                vb[pl.ds(g - STRIDE, STRIDE)]
                + pltpu.roll(vb[pl.ds(g, STRIDE)], 32, 1)
                + pltpu.roll(vb[pl.ds(g + STRIDE, STRIDE)], 64, 1)
            ).astype(BF)

        lhs = jnp.concatenate(
            [va[0:size], va[48 : 48 + size], va[96 : 96 + size], bc[48 : 48 + size]], axis=1
        )
        pbuf[48 : 48 + size] = lax.dot_general(lhs, wb[wi], NT, preferred_element_type=F32)

        @pl.loop(0, n + 1)
        def _(m):
            g = pl.multiple_of(STRIDE * m + STRIDE, STRIDE)
            x = pbuf[pl.ds(g - 8, STRIDE + 16)]
            mid = slice(8, 8 + STRIDE)
            p_b = x[:, 384:512]
            out_a = (
                x[mid, 128:256]
                + pltpu.roll(x[:, 0:128], 1, 0)[mid]
                + pltpu.roll(x[:, 256:384], STRIDE + 15, 0)[mid]
            )
            out_b = (
                pltpu.roll(p_b, 1, 0)[mid]
                + pltpu.roll(p_b[mid], 96, 1)
                + pltpu.roll(pltpu.roll(p_b, STRIDE + 15, 0)[mid], 64, 1)
            )
            epilogue(m, g, out_a, out_b)

    def replicate():
        first = iota((16, 128), 0) < 8
        for ref in (va, vb):
            own, nxt = ref[48:64], ref[96:112]
            ref[0:16] = own
            ref[16:48] = ref[64:96]
            ref[48:64] = jnp.where(first, nxt.astype(F32), own.astype(F32)).astype(ref.dtype)

    def gelu(x):
        return jax.nn.gelu(x, approximate=True)

    def hidden(m, g, o_a, o_b):
        put(g, gelu(o_a), gelu(o_b))

    def first_state(m, g, o_a, o_b):
        s_a = (st_a[pl.ds(g, STRIDE)] + o_a).astype(BF).astype(F32)
        s_b = (st_b[pl.ds(g, STRIDE)] + o_b).astype(BF).astype(F32)
        st_a[pl.ds(g, STRIDE)] = s_a
        st_b[pl.ds(g, STRIDE)] = s_b
        put(g, *normed(s_a, s_b, gain_a, gain_b))

    def second_state(m, g, o_a, o_b):
        s_a, s_b = st_a[pl.ds(g, STRIDE)], st_b[pl.ds(g, STRIDE)]
        t_a = (s_a + o_a).astype(BF)
        t_b = (s_b + o_b).astype(BF)

        @pl.when(m < 16)
        def _():
            r = pl.multiple_of(32 * m, 32)
            fin[0, pl.ds(r, 32), 0:128] = t_a[16:48]
            fin[0, pl.ds(r, 32), 128:256] = t_b[16:48]

        y_a, y_b = oc_a[pl.ds(g, STRIDE)], oc_b[pl.ds(g, STRIDE)]
        mask = y_b[:, 32:33]
        put(
            g,
            (y_a + 0.5 * (s_a + t_a.astype(F32))) * mask,
            (y_b + 0.5 * (s_b + t_b.astype(F32))) * mask,
        )

    def mixed(m, g, o_a, o_b):
        n_a, n_b = normed(
            o_a.astype(BF).astype(F32), o_b.astype(BF).astype(F32), ocean_a, ocean_b
        )

        @pl.when(m < 16)
        def _():
            r = pl.multiple_of(32 * m, 32)
            nrm[pl.ds(r, 32), 0:128] = n_a[16:48].astype(BF)
            nrm[pl.ds(r, 32), 128:256] = n_b[16:48].astype(BF)

    convolve(20, 0, hidden)
    replicate()
    loads[4].wait()
    pair[3].wait_recv()
    prepare(1)
    convolve(19, 1, first_state)
    replicate()
    convolve(18, 0, hidden)
    replicate()
    convolve(17, 1, second_state)
    replicate()
    loads[5].wait()
    pair[4].wait_recv()
    prepare(2)
    convolve(16, 2, mixed)

    loads[6].wait()
    loads[7].wait()

    @pl.loop(0, 2)
    def _(m):
        r = pl.multiple_of(256 * m, 256)
        h = jnp.dot(nrm[pl.ds(r, 256), :][:, :160], miv[...], preferred_element_type=F32)
        h = gelu(h).astype(BF)
        u = lax.dot_general(h, mov[...], NT, preferred_element_type=F32).astype(BF)
        fin[1, pl.ds(r, 256), 0:160] = u

    for b in range(2):
        q = pl.multiple_of(256 * jnp.where(c == 0, b, 3 - b), 256)
        o = pl.multiple_of(256 * jnp.where(c == 0, b, 1 - b), 256)
        t_a = lax.dot_general(
            fin[0, 256 * b : 256 * b + 256][:, :160], tsel[b], TN, preferred_element_type=F32
        )
        u = lax.dot_general(
            fin[1, 256 * b : 256 * b + 256][:, :160], tsel[b], TN, preferred_element_type=F32
        )
        w_row = wet[:, pl.ds(q, 256)].astype(F32)
        for k in range(2):
            rows = slice(80 * k, 80 * k + 80)
            obuf[0, k, :, pl.ds(o, 256)] = t_a[rows].astype(BF)
            obuf[1, k, :, pl.ds(o, 256)] = (
                xo[k, :, pl.ds(q, 256)].astype(F32) + w_row * u[rows]
            ).astype(BF)

    mine = pl.ds(pl.multiple_of(512 * c, 512), 512)
    outs = []
    for n, ref in enumerate((out_a, out_o)):
        outs.append(
            pltpu.make_async_remote_copy(
                src_ref=obuf.at[n, pc],
                dst_ref=ref.at[:, mine],
                send_sem=osem_s.at[n],
                recv_sem=osem_r.at[n],
                device_id=partner,
                device_id_type=MESH,
            )
        )
    for copy in outs:
        copy.start()
    out_a[:, mine] = obuf[0, c]
    out_o[:, mine] = obuf[1, c]
    for copy in halo_copies:
        copy.wait_send()
    for copy in pair:
        copy.wait_send()
    for copy in outs:
        copy.wait()


def per_device(
    atm_state, ocean_state, wet_mask, neighbours, west_rim, east_rim, atm_gain,
    atm_conv_in, atm_conv_out, ocean_conv, ocean_gain, mlp_in, mlp_out,
):
    vmem = pl.BlockSpec(memory_space=pltpu.VMEM)
    anym = pl.BlockSpec(memory_space=pl.ANY)
    pixels = atm_state.shape[1]
    taps = [jnp.transpose(w, (1, 0, 2)) for w in (atm_conv_in, atm_conv_out, ocean_conv)]
    out = jax.ShapeDtypeStruct((CH, pixels), BF)
    dma = pltpu.SemaphoreType.DMA
    return pl.pallas_call(
        kernel,
        name="coupled_step",
        out_shape=(out, out),
        in_specs=[anym] + [vmem] * 3 + [anym] * 7,
        out_specs=(vmem, vmem),
        scratch_shapes=[
            pltpu.VMEM((2, CH, pixels), BF),
            pltpu.VMEM((2, CH, pixels), BF),
            pltpu.VMEM((3, 2, 9, CH, C), BF),
            pltpu.VMEM((3, 512, 512), BF),
            pltpu.VMEM((C, 640), BF),
            pltpu.VMEM((C, 640), BF),
            pltpu.VMEM((2, 8, pixels), jnp.int32),
            pltpu.VMEM((3, 256, 256), BF),
            pltpu.VMEM((2, 2, 96, 128), BF),
            pltpu.VMEM((2, 96, 256), BF),
            pltpu.VMEM((BUF, 128), F32),
            pltpu.VMEM((BUF, 128), F32),
            pltpu.VMEM((BUF, 128), F32),
            pltpu.VMEM((BUF, 128), F32),
            pltpu.VMEM((BUF, 128), BF),
            pltpu.VMEM((BUF, 128), F32),
            pltpu.VMEM((BUF, 128), BF),
            pltpu.VMEM((BUF, 512), F32),
            pltpu.VMEM((512, 256), BF),
            pltpu.VMEM((2, 512, 256), BF),
            pltpu.VMEM((2, 2, CH, 512), BF),
            pltpu.VMEM((8, pixels), jnp.int32),
            dma((8,)),
            dma((5,)),
            dma((5,)),
            dma((4,)),
            dma((2, 2)),
            dma((2,)),
            dma((2,)),
        ],
        compiler_params=pltpu.CompilerParams(
            collective_id=0, has_side_effects=True, vmem_limit_bytes=48 * 1024 * 1024
        ),
    )(
        neighbours,
        wet_mask.reshape(1, pixels),
        atm_gain.reshape(1, C),
        ocean_gain.reshape(1, C),
        atm_state,
        ocean_state,
        *taps,
        jnp.transpose(mlp_in),
        mlp_out,
    )


def solution(mesh):
    in_specs = (
        P("chan", "sector"),
        P("chan", "sector"),
        P("sector"),
        P(None, "sector"),
        P("sector"),
        P("sector"),
        P(),
        P("chan", None, None),
        P("chan", None, None),
        P("chan", None, None),
        P(),
        P(),
        P(),
    )
    out_specs = (P("chan", "sector"), P("chan", "sector"))
    return jax.shard_map(
        per_device, mesh=mesh, in_specs=in_specs, out_specs=out_specs, check_vma=False
    )
```

time: 334 us -> 61 us (0.18)
  local copies, waits for them, and re-layouts: 205 us -> 9.43 us
  Pallas kernels: 0 us -> 50.4 us
  starting transfers between devices: 40.4 us -> 0 us
  blocking collectives: 30.5 us -> 0 us
  waiting for transfers between devices: 27.7 us -> 0 us
  matrix products: 22.7 us -> 0 us
  other arithmetic: 3.5 us -> 0 us
    gather x60 -> x0, local copies, waits for them, and re-layouts: 187 us -> none  [the longest x40 179 us: stencil(): moved = jnp.take(padded, neighbours[neighbour], axis=1)]
    pallas_call x0 -> x1, Pallas kernels: none -> 50.4 us  [per_device(): pl.pallas_call(kernel, name='coupled_step', out_shape=(out, out), in_spec...]
    ppermute x10 -> x0, starting transfers between devices: 40.4 us -> none  [the longest x5 25.5 us: padded_2(): lax.ppermute(lax.slice_in_dim(block, 0, width, axis=dim), axis, backward)]
    ppermute x10 -> x0, waiting for transfers between devices: 27.7 us -> none  [the longest x5 27.1 us: padded_2(): lax.ppermute(lax.slice_in_dim(block, block.shape[dim] - width, None, axis...]
    dot_general x46 -> x0, matrix products: 22.7 us -> none  [the longest x40 20.9 us: stencil(): jnp.dot(weight[:, neighbour + 1, :], moved, preferred_element_type=jnp.fl...]
    all_gather x5 -> x0, blocking collectives: 21.5 us -> none  [gathered(): return lax.all_gather(values_in, 'chan', axis=0, tiled=True)]
    all_to_all x2 -> x0, blocking collectives: 8.99 us -> none  [the longest x1 5.14 us: ocean_mix(): lax.all_to_all(row_block, 'chan', split_axis=1, concat_axis=0, tiled=True)]
    unnamed x220 -> x24, local copies, waits for them, and re-layouts: 15 us -> 9.43 us
  transfers between devices with their start and end apart: 10 -> 0, of which waited for: 5 -> 0; matrix products, arithmetic and copies ran while one was open for 1% -> 0% of each run, Pallas kernels for 0% -> 0%
where the time goes in v1:
time: 61 us; the launch traced here: 60.5 us
  Pallas kernels  50.4 us (83%)
  local copies, waits for them, and re-layouts  9.43 us (15%)
  between operations  0.68 us (1%)
    pallas_call x1, Pallas kernels, per_device(): pl.pallas_call(kernel, name='coupled_step', out_shape=(out, out), in_spec...  50.4 us
    unnamed x24, local copies, waits for them, and re-layouts  9.43 us

profile of v1, /device:TPU:1, one launch (start us, length us, event | category | flops | bytes accessed | tf_op | source)
XLA Modules:
  0.0 60.5 jit_solution(4591801738761573142)
XLA Ops:
  0.6 0.0 copy-start.8
  0.6 0.0 copy-start.10
  0.7 0.0 copy-start.9
  0.7 0.7 %copy-done.8 = s32[1024]{0:T(1024)S(1)} copy-done((s32[1024]{0:T(1024)S(1)}, s32[1024]{0:T(1024)}, u32[]{:S(2)}) %copy-start.8) | copy-done | bytes 4120
  1.3 0.0 copy-done.10
  1.3 0.0 copy-done.9
  1.3 0.0 copy-start
  1.3 1.0 %copy-done = bf16[80,9,160]{2,0,1:T(8,128)(2,1)S(1)} copy-done((bf16[80,9,160]{2,0,1:T(8,128)(2,1)S(1)}, bf16[80,9,160]{2,0,1:T(8,128)(2,1)}, u32[]{:S(2)}) %copy-start) | copy-done | bytes 230424
  2.3 0.0 copy-start.1
  2.3 1.0 %copy-done.1 = bf16[80,9,160]{2,0,1:T(8,128)(2,1)S(1)} copy-done((bf16[80,9,160]{2,0,1:T(8,128)(2,1)S(1)}, bf16[80,9,160]{2,0,1:T(8,128)(2,1)}, u32[]{:S(2)}) %copy-start.1) | copy-done | bytes 230424
  3.3 0.0 copy-start.2
  3.3 1.0 %copy-done.2 = bf16[80,9,160]{2,0,1:T(8,128)(2,1)S(1)} copy-done((bf16[80,9,160]{2,0,1:T(8,128)(2,1)S(1)}, bf16[80,9,160]{2,0,1:T(8,128)(2,1)}, u32[]{:S(2)}) %copy-start.2) | copy-done | bytes 230424
  4.3 0.0 copy-start.3
  4.3 0.9 %copy-done.3 = bf16[640,160]{0,1:T(8,128)(2,1)S(1)} copy-done((bf16[640,160]{0,1:T(8,128)(2,1)S(1)}, bf16[640,160]{0,1:T(8,128)(2,1)}, u32[]{:S(2)}) %copy-start.3) | copy-done | bytes 204824
  5.2 0.0 copy-start.4
  5.2 0.9 %copy-done.4 = bf16[160,640]{1,0:T(8,128)(2,1)S(1)} copy-done((bf16[160,640]{1,0:T(8,128)(2,1)S(1)}, bf16[160,640]{1,0:T(8,128)(2,1)}, u32[]{:S(2)}) %copy-start.4) | copy-done | bytes 204824
  6.2 0.0 copy-start.5
  6.2 0.9 %copy-done.5 = bf16[80,1024]{1,0:T(8,128)(2,1)S(1)} copy-done((bf16[80,1024]{1,0:T(8,128)(2,1)S(1)}, bf16[80,1024]{1,0:T(8,128)(2,1)}, u32[]{:S(2)}) %copy-start.5) | copy-done | bytes 163864
  7.1 0.0 copy-start.6
  7.1 0.9 %copy-done.6 = bf16[80,1024]{1,0:T(8,128)(2,1)S(1)} copy-done((bf16[80,1024]{1,0:T(8,128)(2,1)S(1)}, bf16[80,1024]{1,0:T(8,128)(2,1)}, u32[]{:S(2)}) %copy-start.6) | copy-done | bytes 163864
  8.0 0.0 copy-start.7
  8.0 0.8 %copy-done.7 = s32[8,1024]{1,0:T(8,128)S(1)} copy-done((s32[8,1024]{1,0:T(8,128)S(1)}, s32[8,1024]{1,0:T(8,128)}, u32[]{:S(2)}) %copy-start.7) | copy-done | bytes 32792
  8.8 50.4 %coupled_step.1 = (bf16[80,1024]{1,0:T(8,128)(2,1)S(1)}, bf16[80,1024]{1,0:T(8,128)(2,1)S(1)}) custom-call(s32[8,1024]{1,0:T(8,128)S(1)} %copy-done.7, s32[1,1024]{1,0:T(1,128)S(1)} %bitcast.11, f32[1,160]{1,0:T(1,128)S(1)} %bitcast.12, f32[1,160]{1,0:T(1,128)S(1)} %bitcast.13, bf16[80,1024]{1,0:T(8,128)(2,1)S(1)} %copy-done.5, ...), custom_call_target="tpu_custom_call" | custom-call | tf_op jit(solution)/shard_map/coupled_step/pallas_call | solution.py:447
  59.2 0.7 %copy.15 = bf16[80,1024]{1,0:T(8,128)(2,1)} copy(bf16[80,1024]{1,0:T(8,128)(2,1)S(1)} %get-tuple-element.4) | data formatting | bytes 327680
  59.9 0.7 %copy.16 = bf16[80,1024]{1,0:T(8,128)(2,1)} copy(bf16[80,1024]{1,0:T(8,128)(2,1)S(1)} %get-tuple-element.5) | data formatting | bytes 327680
Async XLA Ops:
  0.6 0.7 %copy-start.8 = (s32[1024]{0:T(1024)S(1)}, s32[1024]{0:T(1024)}, u32[]{:S(2)}) copy-start(s32[1024]{0:T(1024)} %param.15) | copy-start | bytes 12292
  0.6 0.7 %copy-start.10 = (f32[160]{0:T(256)S(1)}, f32[160]{0:T(256)}, u32[]{:S(2)}) copy-start(f32[160]{0:T(256)} %param.21) | copy-start | bytes 1924
  0.7 0.7 %copy-start.9 = (f32[160]{0:T(256)S(1)}, f32[160]{0:T(256)}, u32[]{:S(2)}) copy-start(f32[160]{0:T(256)} %param.17) | copy-start | bytes 1924
  1.3 1.0 %copy-start = (bf16[80,9,160]{2,0,1:T(8,128)(2,1)S(1)}, bf16[80,9,160]{2,0,1:T(8,128)(2,1)}, u32[]{:S(2)}) copy-start(bf16[80,9,160]{2,0,1:T(8,128)(2,1)} %param.18) | copy-start | bytes 691204
  2.3 1.0 %copy-start.1 = (bf16[80,9,160]{2,0,1:T(8,128)(2,1)S(1)}, bf16[80,9,160]{2,0,1:T(8,128)(2,1)}, u32[]{:S(2)}) copy-start(bf16[80,9,160]{2,0,1:T(8,128)(2,1)} %param.19) | copy-start | bytes 691204
  3.3 1.0 %copy-start.2 = (bf16[80,9,160]{2,0,1:T(8,128)(2,1)S(1)}, bf16[80,9,160]{2,0,1:T(8,128)(2,1)}, u32[]{:S(2)}) copy-start(bf16[80,9,160]{2,0,1:T(8,128)(2,1)} %param.20) | copy-start | bytes 691204
  4.3 0.9 %copy-start.3 = (bf16[640,160]{0,1:T(8,128)(2,1)S(1)}, bf16[640,160]{0,1:T(8,128)(2,1)}, u32[]{:S(2)}) copy-start(bf16[640,160]{0,1:T(8,128)(2,1)} %param.22) | copy-start | bytes 614404
  5.2 0.9 %copy-start.4 = (bf16[160,640]{1,0:T(8,128)(2,1)S(1)}, bf16[160,640]{1,0:T(8,128)(2,1)}, u32[]{:S(2)}) copy-start(bf16[160,640]{1,0:T(8,128)(2,1)} %mo.1) | copy-start | bytes 614404
  6.2 0.9 %copy-start.5 = (bf16[80,1024]{1,0:T(8,128)(2,1)S(1)}, bf16[80,1024]{1,0:T(8,128)(2,1)}, u32[]{:S(2)}) copy-start(bf16[80,1024]{1,0:T(8,128)(2,1)} %atm.1) | copy-start | bytes 491524
  7.1 0.9 %copy-start.6 = (bf16[80,1024]{1,0:T(8,128)(2,1)S(1)}, bf16[80,1024]{1,0:T(8,128)(2,1)}, u32[]{:S(2)}) copy-start(bf16[80,1024]{1,0:T(8,128)(2,1)} %oc.1) | copy-start | bytes 491524
  8.0 0.8 %copy-start.7 = (s32[8,1024]{1,0:T(8,128)S(1)}, s32[8,1024]{1,0:T(8,128)}, u32[]{:S(2)}) copy-start(s32[8,1024]{1,0:T(8,128)} %nb.1) | copy-start | bytes 98308

commit v2 on v1

--- a/solution.py
+++ b/solution.py
@@ -13,6 +13,7 @@
 ROWS = 32
 STRIDE = 48
 BUF = 1104
+BC = BUF + 96
 MESH = pl.DeviceIdType.MESH
 NT = (((1,), (1,)), ((), ()))
 TN = (((0,), (0,)), ((), ()))
@@ -37,7 +38,7 @@
     nb, wet, ga, go, atm, oc, w1, w2, w3, mi, mo,
     out_a, out_o,
     xa, xo, wraw, wb, miv, mov, keys, tsel, sbuf, halo, st_a, st_b, oc_a, oc_b,
-    va, vb, bc, pbuf, nrm, fin, obuf, nbv,
+    va, bc, pbuf, nrm, fin, obuf, nbv,
     lsem, psem_s, psem_r, hsem_s, hsem_r, osem_s, osem_r,
 ):
     sectors = lax.axis_size("sector")
@@ -181,21 +182,22 @@
     prepare(0)
 
     gain_a = ga[:, 0:128]
-    gain_b = jnp.concatenate([ga[:, 128:160], jnp.zeros((1, 96), F32)], axis=1)
+    gain_b = jnp.concatenate([ga[:, 128:160]] * 4, axis=1)
     ocean_a = go[:, 0:128]
-    ocean_b = jnp.concatenate([go[:, 128:160], jnp.zeros((1, 96), F32)], axis=1)
+    ocean_b = jnp.concatenate([go[:, 128:160]] * 4, axis=1)
 
     pair[0].wait_recv()
     pair[2].wait_recv()
     for b in range(3):
         q = pl.multiple_of(256 * jnp.where(c == 0, b, 3 - b), 256)
+        x_1 = xa[1, :, pl.ds(q, 256)]
         x_a = jnp.concatenate(
-            [xa[0, :, pl.ds(q, 256)], xa[1, :, pl.ds(q, 256)], jnp.zeros((96, 256), BF)], axis=0
-        )
-        wet_b = jnp.broadcast_to(wet[:, pl.ds(q, 256)], (16, 256)).astype(F32).astype(BF)
+            [xa[0, :, pl.ds(q, 256)], x_1] + [x_1[48:80]] * 3, axis=0
+        )
+        wet_b = jnp.broadcast_to(wet[:, pl.ds(q, 256)], (32, 256)).astype(F32).astype(BF)
+        x_1 = xo[1, :, pl.ds(q, 256)]
         x_o = jnp.concatenate(
-            [xo[0, :, pl.ds(q, 256)], xo[1, :, pl.ds(q, 256)], wet_b, jnp.zeros((80, 256), BF)],
-            axis=0,
+            [xo[0, :, pl.ds(q, 256)], x_1] + [x_1[48:80]] * 2 + [wet_b], axis=0
         )
         v_a = lax.dot_general(tsel[b], x_a, NT, preferred_element_type=F32)
         v_o = lax.dot_general(tsel[b], x_o, NT, preferred_element_type=F32)
@@ -220,8 +222,10 @@
                 device_id=partner,
                 device_id_type=MESH,
             ).wait_recv()
-    h_all = jnp.concatenate(
-        [halo[0, 0:80], halo[1, 0:80], halo[0, 80:96], jnp.zeros((80, 256), BF)], axis=0
+    h_1 = halo[1, 48:80]
+    h_atm = jnp.concatenate([halo[0, 0:80], halo[1, 0:80]] + [h_1] * 3, axis=0)
+    h_oc = jnp.concatenate(
+        [halo[0, 0:80], halo[1, 0:80]] + [h_1] * 2 + [halo[0, 80:96]] * 2, axis=0
     )
     hl = iota((1, 256), 1)
     hh = hl & 127
@@ -232,7 +236,7 @@
     p2 = jnp.where(hi == 0, p1 - 16, p1)
     r = iota((368, 256), 0)
     v_a = lax.dot_general(
-        onehot((r == p1) | (r == p2)), h_all, NT, preferred_element_type=F32
+        onehot((r == p1) | (r == p2)), h_atm, NT, preferred_element_type=F32
     )
     oi = hh - 105
     p1 = jnp.where(
@@ -241,7 +245,7 @@
     p2 = jnp.where(oi == 0, p1 - 16, p1)
     r = iota((304, 256), 0)
     v_o = lax.dot_general(
-        onehot((r == p1) | (r == p2)), h_all, NT, preferred_element_type=F32
+        onehot((r == p1) | (r == p2)), h_oc, NT, preferred_element_type=F32
     )
     for k in range(23):
         rows = slice(16 * k, 16 * k + 16)
@@ -252,51 +256,37 @@
             oc_a[g : g + 16] = v_o[rows, :128]
             oc_b[g : g + 16] = v_o[rows, 128:]
 
-    low = iota((STRIDE, 128), 1) < 32
+    group = lax.shift_right_logical(iota((1, 128), 1), 5)
 
     def normed(x_a, x_b, scale_a, scale_b):
-        x_b = jnp.where(low, x_b, 0.0)
-        mean_sq = jnp.sum(x_a * x_a + x_b * x_b, axis=1, keepdims=True) * (1.0 / C)
+        mean_sq = jnp.sum(x_a * x_a + 0.25 * (x_b * x_b), axis=1, keepdims=True) * (1.0 / C)
         inv = lax.rsqrt(mean_sq + EPSILON)
         return x_a * inv * scale_a, x_b * inv * scale_b
 
-    def put(g, x_a, x_b):
-        va[pl.ds(g, STRIDE)] = x_a.astype(BF)
-        vb[pl.ds(g, STRIDE)] = jnp.where(low, x_b, 0.0).astype(BF).astype(F32)
-
-    @pl.loop(0, 22)
+    def put(g, x_a, x_b, rows=STRIDE):
+        va[pl.ds(g, rows)] = x_a.astype(BF)
+        y = x_b.astype(BF)
+        bc[pl.ds(g + 2 * STRIDE, rows), 0:32] = y[:, 0:32]
+        bc[pl.ds(g + STRIDE, rows), 32:64] = y[:, 32:64]
+        bc[pl.ds(g, rows), 64:96] = y[:, 64:96]
+
+    bc[:, 96:128] = jnp.zeros((BC, 32), BF)
+
+    @pl.loop(0, 22, unroll=True)
     def _(m):
         g = pl.multiple_of(STRIDE * m, STRIDE)
-        x_a, x_b = normed(
-            st_a[pl.ds(g, STRIDE)], st_b[pl.ds(g, STRIDE)], gain_a, gain_b
-        )
-        put(g, x_a, x_b)
-
-    top = slice(1056, 1072)
-    x_a, x_b = st_a[top], st_b[top]
-    mean_sq = jnp.sum(x_a * x_a + x_b * x_b, axis=1, keepdims=True) * (1.0 / C)
-    inv = lax.rsqrt(mean_sq + EPSILON)
-    va[top] = (x_a * inv * gain_a).astype(BF)
-    vb[top] = (x_b * inv * gain_b).astype(BF).astype(F32)
+        put(g, *normed(st_a[pl.ds(g, STRIDE)], st_b[pl.ds(g, STRIDE)], gain_a, gain_b))
+
+    put(1056, *normed(st_a[1056:1072], st_b[1056:1072], gain_a, gain_b), rows=16)
 
     def convolve(n, wi, epilogue):
         size = 16 + STRIDE * n
-
-        @pl.loop(0, n + 1)
-        def _(m):
-            g = pl.multiple_of(STRIDE * m + STRIDE, STRIDE)
-            bc[pl.ds(g, STRIDE)] = (
-                vb[pl.ds(g - STRIDE, STRIDE)]
-                + pltpu.roll(vb[pl.ds(g, STRIDE)], 32, 1)
-                + pltpu.roll(vb[pl.ds(g + STRIDE, STRIDE)], 64, 1)
-            ).astype(BF)
-
         lhs = jnp.concatenate(
-            [va[0:size], va[48 : 48 + size], va[96 : 96 + size], bc[48 : 48 + size]], axis=1
+            [va[0:size], va[48 : 48 + size], va[96 : 96 + size], bc[96 : 96 + size]], axis=1
         )
         pbuf[48 : 48 + size] = lax.dot_general(lhs, wb[wi], NT, preferred_element_type=F32)
 
-        @pl.loop(0, n + 1)
+        @pl.loop(0, n + 1, unroll=True)
         def _(m):
             g = pl.multiple_of(STRIDE * m + STRIDE, STRIDE)
             x = pbuf[pl.ds(g - 8, STRIDE + 16)]
@@ -307,20 +297,29 @@
                 + pltpu.roll(x[:, 0:128], 1, 0)[mid]
                 + pltpu.roll(x[:, 256:384], STRIDE + 15, 0)[mid]
             )
-            out_b = (
-                pltpu.roll(p_b, 1, 0)[mid]
-                + pltpu.roll(p_b[mid], 96, 1)
-                + pltpu.roll(pltpu.roll(p_b, STRIDE + 15, 0)[mid], 64, 1)
-            )
-            epilogue(m, g, out_a, out_b)
+            y = jnp.where(group == 0, pltpu.roll(p_b, 1, 0)[mid], 0.0)
+            y = jnp.where(group == 1, p_b[mid], y)
+            y = jnp.where(group == 2, pltpu.roll(p_b, STRIDE + 15, 0)[mid], y)
+            y = y + pltpu.roll(y, 64, 1)
+            epilogue(m, g, out_a, y + pltpu.roll(y, 32, 1))
 
     def replicate():
         first = iota((16, 128), 0) < 8
-        for ref in (va, vb):
-            own, nxt = ref[48:64], ref[96:112]
-            ref[0:16] = own
-            ref[16:48] = ref[64:96]
-            ref[48:64] = jnp.where(first, nxt.astype(F32), own.astype(F32)).astype(ref.dtype)
+
+        def mix(own, nxt):
+            mask = first[:, : own.shape[1]]
+            return jnp.where(mask, nxt.astype(F32), own.astype(F32)).astype(BF)
+
+        for ref, at, lanes in (
+            (va, 0, slice(0, 128)),
+            (bc, 96, slice(0, 32)),
+            (bc, 48, slice(32, 64)),
+            (bc, 0, slice(64, 96)),
+        ):
+            own, nxt = ref[at + 48 : at + 64, lanes], ref[at + 96 : at + 112, lanes]
+            ref[at : at + 16, lanes] = own
+            ref[at + 16 : at + 48, lanes] = ref[at + 64 : at + 96, lanes]
+            ref[at + 48 : at + 64, lanes] = mix(own, nxt)
 
     def gelu(x):
         return jax.nn.gelu(x, approximate=True)
@@ -339,15 +338,11 @@
         s_a, s_b = st_a[pl.ds(g, STRIDE)], st_b[pl.ds(g, STRIDE)]
         t_a = (s_a + o_a).astype(BF)
         t_b = (s_b + o_b).astype(BF)
-
-        @pl.when(m < 16)
-        def _():
-            r = pl.multiple_of(32 * m, 32)
-            fin[0, pl.ds(r, 32), 0:128] = t_a[16:48]
-            fin[0, pl.ds(r, 32), 128:256] = t_b[16:48]
-
+        r = pl.multiple_of(32 * m, 32)
+        fin[0, pl.ds(r, 32), 0:128] = t_a[16:48]
+        fin[0, pl.ds(r, 32), 128:256] = t_b[16:48]
         y_a, y_b = oc_a[pl.ds(g, STRIDE)], oc_b[pl.ds(g, STRIDE)]
-        mask = y_b[:, 32:33]
+        mask = y_b[:, 96:97]
         put(
             g,
             (y_a + 0.5 * (s_a + t_a.astype(F32))) * mask,
@@ -358,12 +353,9 @@
         n_a, n_b = normed(
             o_a.astype(BF).astype(F32), o_b.astype(BF).astype(F32), ocean_a, ocean_b
         )
-
-        @pl.when(m < 16)
-        def _():
-            r = pl.multiple_of(32 * m, 32)
-            nrm[pl.ds(r, 32), 0:128] = n_a[16:48].astype(BF)
-            nrm[pl.ds(r, 32), 128:256] = n_b[16:48].astype(BF)
+        r = pl.multiple_of(32 * m, 32)
+        nrm[pl.ds(r, 32), 0:128] = n_a[16:48].astype(BF)
+        nrm[pl.ds(r, 32), 128:256] = n_b[16:48].astype(BF)
 
     convolve(20, 0, hidden)
     replicate()
@@ -466,11 +458,10 @@
             pltpu.VMEM((BUF, 128), F32),
             pltpu.VMEM((BUF, 128), F32),
             pltpu.VMEM((BUF, 128), BF),
-            pltpu.VMEM((BUF, 128), F32),
-            pltpu.VMEM((BUF, 128), BF),
+            pltpu.VMEM((BC, 128), BF),
             pltpu.VMEM((BUF, 512), F32),
-            pltpu.VMEM((512, 256), BF),
-            pltpu.VMEM((2, 512, 256), BF),
+            pltpu.VMEM((576, 256), BF),
+            pltpu.VMEM((2, 576, 256), BF),
             pltpu.VMEM((2, 2, CH, 512), BF),
             pltpu.VMEM((8, pixels), jnp.int32),
             dma((8,)),
@@ -482,7 +473,7 @@
             dma((2,)),
         ],
         compiler_params=pltpu.CompilerParams(
-            collective_id=0, has_side_effects=True, vmem_limit_bytes=48 * 1024 * 1024
+            collective_id=0, has_side_effects=True, vmem_limit_bytes=67_043_328
         ),
     )(
         neighbours,

time: 61 us -> 33.9 us (0.56)
  Pallas kernels: 50.4 us -> 30.8 us
  local copies, waits for them, and re-layouts: 9.43 us -> 2.3 us
    pallas_call x1, Pallas kernels: 50.4 us -> 30.8 us  [per_device(): pl.pallas_call(kernel, name='coupled_step', out_shape=(out, out), in_spec...]
    unnamed x24 -> x4, local copies, waits for them, and re-layouts: 9.43 us -> 2.3 us
where the time goes in v2:
time: 33.9 us; the launch traced here: 33.7 us
  Pallas kernels  30.8 us (91%)
  local copies, waits for them, and re-layouts  2.3 us (7%)
  between operations  0.65 us (2%)
    pallas_call x1, Pallas kernels, per_device(): pl.pallas_call(kernel, name='coupled_step', out_shape=(out, out), in_spec...  30.8 us
    unnamed x4, local copies, waits for them, and re-layouts  2.3 us

profile of v2, /device:TPU:1, one launch (start us, length us, event | category | flops | bytes accessed | tf_op | source)
XLA Modules:
  0.0 33.7 jit_solution(16204969078367879648)
XLA Ops:
  0.6 30.8 %coupled_step.1 = (bf16[80,1024]{1,0:T(8,128)(2,1)}, bf16[80,1024]{1,0:T(8,128)(2,1)}) custom-call(s32[8,1024]{1,0:T(8,128)} %nb.1, s32[1,1024]{1,0:T(1,128)} %bitcast.11, f32[1,160]{1,0:T(1,128)} %bitcast.12, f32[1,160]{1,0:T(1,128)} %bitcast.13, bf16[80,1024]{1,0:T(8,128)(2,1)} %atm.1, bf16[80,1024]{1,0:T(8,128)(2,1)} %oc.1, bf16[9,80,160]{2,1,0:T(8,128)(2,1)} %bitcast.7, ...), custom_call_target="tpu_custom_call" | custom-call | tf_op jit(solution)/shard_map/coupled_step/pallas_call | solution.py:439
  31.4 0.0 copy-start
  31.4 1.6 %copy.15 = bf16[80,1024]{1,0:T(8,128)(2,1)} copy(bf16[80,1024]{1,0:T(8,128)(2,1)} %get-tuple-element.4) | data formatting | bytes 327680
  33.1 0.0 copy-done
  33.1 0.7 %copy.16 = bf16[80,1024]{1,0:T(8,128)(2,1)} copy(bf16[80,1024]{1,0:T(8,128)(2,1)S(1)} %copy-done) | data formatting | bytes 327680
Async XLA Ops:
  31.4 1.6 %copy-start = (bf16[80,1024]{1,0:T(8,128)(2,1)S(1)}, bf16[80,1024]{1,0:T(8,128)(2,1)}, u32[]{:S(2)}) copy-start(bf16[80,1024]{1,0:T(8,128)(2,1)} %get-tuple-element.5) | copy-start | bytes 491524

commit v3 on v2

--- a/solution.py
+++ b/solution.py
@@ -14,6 +14,8 @@
 STRIDE = 48
 BUF = 1104
 BC = BUF + 96
+GROUP = 10
+AHEAD = 2
 MESH = pl.DeviceIdType.MESH
 NT = (((1,), (1,)), ((), ()))
 TN = (((0,), (0,)), ((), ()))
@@ -35,10 +37,10 @@
 
 
 def kernel(
-    nb, wet, ga, go, atm, oc, w1, w2, w3, mi, mo,
+    nb, wet_h, ga_h, go_h, atm, oc, w1, w2, w3, mi, mo,
     out_a, out_o,
     xa, xo, wraw, wb, miv, mov, keys, tsel, sbuf, halo, st_a, st_b, oc_a, oc_b,
-    va, bc, pbuf, nrm, fin, obuf, nbv,
+    va, bc, pbuf, nrm, fin, obuf, nbv, wet, ga, go, hsel, osel,
     lsem, psem_s, psem_r, hsem_s, hsem_r, osem_s, osem_r,
 ):
     sectors = lax.axis_size("sector")
@@ -66,6 +68,9 @@
         pltpu.make_async_copy(w3, wraw.at[2, c], lsem.at[5]),
         pltpu.make_async_copy(mi, miv, lsem.at[6]),
         pltpu.make_async_copy(mo, mov, lsem.at[7]),
+        pltpu.make_async_copy(wet_h, wet, lsem.at[8]),
+        pltpu.make_async_copy(ga_h, ga, lsem.at[9]),
+        pltpu.make_async_copy(go_h, go, lsem.at[10]),
     ]
     for load in loads:
         load.start()
@@ -86,6 +91,7 @@
 
     loads[1].wait()
     loads[2].wait()
+    loads[8].wait()
 
     wet16 = jnp.broadcast_to(wet[...], (16, 1024)).astype(F32).astype(BF)
 
@@ -177,40 +183,87 @@
                     r = 384 + 32 * dxi
                     wb[n, r : r + 32, dst : dst + width] = w_1[48:80, lanes]
 
-    loads[3].wait()
-    pair[1].wait_recv()
-    prepare(0)
-
+    hl = iota((1, 256), 1)
+    hh = hl & 127
+    far = hl >= 128
+    hi = lax.shift_right_logical(hh * 205, 10)
+    he = hh - 5 * hi
+    p1 = jnp.where(hh < 105, jnp.where(far, 16 * hi + 27 + he, 16 * hi + 32 + he), -1)
+    p2 = jnp.where(hi == 0, p1 - 16, p1)
+    r = iota((368, 256), 0)
+    hsel[...] = onehot((r == p1) | (r == p2))
+    oi = hh - 105
+    p1 = jnp.where((oi >= 0) & (oi < 17), jnp.where(far, 16 * oi + 31, 16 * oi + 32), -1)
+    p2 = jnp.where(oi == 0, p1 - 16, p1)
+    r = iota((304, 256), 0)
+    osel[...] = onehot((r == p1) | (r == p2))
+
+    loads[9].wait()
+    loads[10].wait()
     gain_a = ga[:, 0:128]
     gain_b = jnp.concatenate([ga[:, 128:160]] * 4, axis=1)
     ocean_a = go[:, 0:128]
     ocean_b = jnp.concatenate([go[:, 128:160]] * 4, axis=1)
 
+    def normed(x_a, x_b, scale_a, scale_b):
+        mean_sq = jnp.sum(x_a * x_a + 0.25 * (x_b * x_b), axis=1, keepdims=True) * (1.0 / C)
+        inv = lax.rsqrt(mean_sq + EPSILON)
+        return x_a * inv * scale_a, x_b * inv * scale_b
+
+    def put(v, g, x_a, x_b, rows=STRIDE):
+        va[v, pl.ds(g, rows)] = x_a.astype(BF)
+        y = x_b.astype(BF)
+        bc[v, pl.ds(g + 2 * STRIDE, rows), 0:32] = y[:, 0:32]
+        bc[v, pl.ds(g + STRIDE, rows), 32:64] = y[:, 32:64]
+        bc[v, pl.ds(g, rows), 64:96] = y[:, 64:96]
+
+    for v in range(2):
+        bc[v, :, 96:128] = jnp.zeros((BC, 32), BF)
+
     pair[0].wait_recv()
+    for b in range(3):
+        q = pl.multiple_of(256 * jnp.where(c == 0, b, 3 - b), 256)
+        x_1 = xa[1, :, pl.ds(q, 256)]
+        x_a = jnp.concatenate([xa[0, :, pl.ds(q, 256)], x_1] + [x_1[48:80]] * 3, axis=0)
+        v_a = lax.dot_general(tsel[b], x_a, NT, preferred_element_type=F32)
+        for il in range(8):
+            i = 8 * b + il
+            rows = slice(32 * il, 32 * il + 32)
+            if i <= 20:
+                n_a, n_b = normed(v_a[rows, :128], v_a[rows, 128:], gain_a, gain_b)
+            for g in [STRIDE * (i + 1) + 16] + ([16] if i == 0 else []):
+                if i <= 20:
+                    st_a[g : g + 32] = v_a[rows, :128]
+                    st_b[g : g + 32] = v_a[rows, 128:]
+                    put(0, g, n_a, n_b, rows=32)
+
+    loads[3].wait()
+    pair[1].wait_recv()
+    prepare(0)
+
     pair[2].wait_recv()
     for b in range(3):
         q = pl.multiple_of(256 * jnp.where(c == 0, b, 3 - b), 256)
-        x_1 = xa[1, :, pl.ds(q, 256)]
-        x_a = jnp.concatenate(
-            [xa[0, :, pl.ds(q, 256)], x_1] + [x_1[48:80]] * 3, axis=0
-        )
         wet_b = jnp.broadcast_to(wet[:, pl.ds(q, 256)], (32, 256)).astype(F32).astype(BF)
         x_1 = xo[1, :, pl.ds(q, 256)]
         x_o = jnp.concatenate(
             [xo[0, :, pl.ds(q, 256)], x_1] + [x_1[48:80]] * 2 + [wet_b], axis=0
         )
-        v_a = lax.dot_general(tsel[b], x_a, NT, preferred_element_type=F32)
         v_o = lax.dot_general(tsel[b], x_o, NT, preferred_element_type=F32)
         for il in range(8):
             i = 8 * b + il
             rows = slice(32 * il, 32 * il + 32)
             for g in [STRIDE * (i + 1) + 16] + ([16] if i == 0 else []):
-                if i <= 20:
-                    st_a[g : g + 32] = v_a[rows, :128]
-                    st_b[g : g + 32] = v_a[rows, 128:]
                 if i <= 16:
                     oc_a[g : g + 32] = v_o[rows, :128]
                     oc_b[g : g + 32] = v_o[rows, 128:]
+
+    for n in (1, 2):
+        loads[3 + n].wait()
+        pair[2 + n].wait_recv()
+        prepare(n)
+    loads[6].wait()
+    loads[7].wait()
 
     for d in range(2):
         for sender in range(2):
@@ -227,83 +280,59 @@
     h_oc = jnp.concatenate(
         [halo[0, 0:80], halo[1, 0:80]] + [h_1] * 2 + [halo[0, 80:96]] * 2, axis=0
     )
-    hl = iota((1, 256), 1)
-    hh = hl & 127
-    far = hl >= 128
-    hi = lax.shift_right_logical(hh * 205, 10)
-    he = hh - 5 * hi
-    p1 = jnp.where(hh < 105, jnp.where(far, 16 * hi + 27 + he, 16 * hi + 32 + he), -1)
-    p2 = jnp.where(hi == 0, p1 - 16, p1)
-    r = iota((368, 256), 0)
-    v_a = lax.dot_general(
-        onehot((r == p1) | (r == p2)), h_atm, NT, preferred_element_type=F32
-    )
-    oi = hh - 105
-    p1 = jnp.where(
-        (oi >= 0) & (oi < 17), jnp.where(far, 16 * oi + 31, 16 * oi + 32), -1
-    )
-    p2 = jnp.where(oi == 0, p1 - 16, p1)
-    r = iota((304, 256), 0)
-    v_o = lax.dot_general(
-        onehot((r == p1) | (r == p2)), h_oc, NT, preferred_element_type=F32
-    )
+    v_a = lax.dot_general(hsel[...], h_atm, NT, preferred_element_type=F32)
+    v_o = lax.dot_general(osel[...], h_oc, NT, preferred_element_type=F32)
     for k in range(23):
         rows = slice(16 * k, 16 * k + 16)
         g = STRIDE * k
         st_a[g : g + 16] = v_a[rows, :128]
         st_b[g : g + 16] = v_a[rows, 128:]
+        put(0, g, *normed(v_a[rows, :128], v_a[rows, 128:], gain_a, gain_b), rows=16)
         if k < 19:
             oc_a[g : g + 16] = v_o[rows, :128]
             oc_b[g : g + 16] = v_o[rows, 128:]
 
     group = lax.shift_right_logical(iota((1, 128), 1), 5)
 
-    def normed(x_a, x_b, scale_a, scale_b):
-        mean_sq = jnp.sum(x_a * x_a + 0.25 * (x_b * x_b), axis=1, keepdims=True) * (1.0 / C)
-        inv = lax.rsqrt(mean_sq + EPSILON)
-        return x_a * inv * scale_a, x_b * inv * scale_b
-
-    def put(g, x_a, x_b, rows=STRIDE):
-        va[pl.ds(g, rows)] = x_a.astype(BF)
-        y = x_b.astype(BF)
-        bc[pl.ds(g + 2 * STRIDE, rows), 0:32] = y[:, 0:32]
-        bc[pl.ds(g + STRIDE, rows), 32:64] = y[:, 32:64]
-        bc[pl.ds(g, rows), 64:96] = y[:, 64:96]
-
-    bc[:, 96:128] = jnp.zeros((BC, 32), BF)
-
-    @pl.loop(0, 22, unroll=True)
-    def _(m):
-        g = pl.multiple_of(STRIDE * m, STRIDE)
-        put(g, *normed(st_a[pl.ds(g, STRIDE)], st_b[pl.ds(g, STRIDE)], gain_a, gain_b))
-
-    put(1056, *normed(st_a[1056:1072], st_b[1056:1072], gain_a, gain_b), rows=16)
-
-    def convolve(n, wi, epilogue):
-        size = 16 + STRIDE * n
+    def bounds(n):
+        cuts = list(range(0, n, GROUP))
+        if n - cuts[-1] < GROUP // 2:
+            cuts.pop()
+        return list(zip(cuts, cuts[1:] + [n]))
+
+    def products(v, n, wi, lo, hi):
+        a = 48 if lo == 0 else STRIDE * lo + 64
+        z = STRIDE * hi + 64
         lhs = jnp.concatenate(
-            [va[0:size], va[48 : 48 + size], va[96 : 96 + size], bc[96 : 96 + size]], axis=1
-        )
-        pbuf[48 : 48 + size] = lax.dot_general(lhs, wb[wi], NT, preferred_element_type=F32)
-
-        @pl.loop(0, n + 1, unroll=True)
-        def _(m):
-            g = pl.multiple_of(STRIDE * m + STRIDE, STRIDE)
-            x = pbuf[pl.ds(g - 8, STRIDE + 16)]
-            mid = slice(8, 8 + STRIDE)
+            [va[v, a - 48 : z - 48], va[v, a:z], va[v, a + 48 : z + 48], bc[v, a + 48 : z + 48]],
+            axis=1,
+        )
+        pbuf[a:z] = lax.dot_general(lhs, wb[wi], NT, preferred_element_type=F32)
+
+    def finish(v, n, epilogue, lo, hi):
+        def piece(m, g, rows):
+            x = pbuf[pl.ds(g - 8, rows + 16)]
+            mid = slice(8, 8 + rows)
             p_b = x[:, 384:512]
             out_a = (
                 x[mid, 128:256]
                 + pltpu.roll(x[:, 0:128], 1, 0)[mid]
-                + pltpu.roll(x[:, 256:384], STRIDE + 15, 0)[mid]
+                + pltpu.roll(x[:, 256:384], rows + 15, 0)[mid]
             )
             y = jnp.where(group == 0, pltpu.roll(p_b, 1, 0)[mid], 0.0)
             y = jnp.where(group == 1, p_b[mid], y)
-            y = jnp.where(group == 2, pltpu.roll(p_b, STRIDE + 15, 0)[mid], y)
+            y = jnp.where(group == 2, pltpu.roll(p_b, rows + 15, 0)[mid], y)
             y = y + pltpu.roll(y, 64, 1)
-            epilogue(m, g, out_a, y + pltpu.roll(y, 32, 1))
-
-    def replicate():
+            epilogue(v, m, g, rows, out_a, y + pltpu.roll(y, 32, 1))
+
+        @pl.loop(lo, hi, unroll=True)
+        def _(m):
+            piece(m, pl.multiple_of(STRIDE * m + STRIDE, STRIDE), STRIDE)
+
+        if hi == n and n > 16:
+            piece(n, STRIDE * n + STRIDE, 16)
+
+    def replicate(v):
         first = iota((16, 128), 0) < 8
 
         def mix(own, nxt):
@@ -316,40 +345,43 @@
             (bc, 48, slice(32, 64)),
             (bc, 0, slice(64, 96)),
         ):
-            own, nxt = ref[at + 48 : at + 64, lanes], ref[at + 96 : at + 112, lanes]
-            ref[at : at + 16, lanes] = own
-            ref[at + 16 : at + 48, lanes] = ref[at + 64 : at + 96, lanes]
-            ref[at + 48 : at + 64, lanes] = mix(own, nxt)
+            own, nxt = ref[v, at + 48 : at + 64, lanes], ref[v, at + 96 : at + 112, lanes]
+            ref[v, at : at + 16, lanes] = own
+            ref[v, at + 16 : at + 48, lanes] = ref[v, at + 64 : at + 96, lanes]
+            ref[v, at + 48 : at + 64, lanes] = mix(own, nxt)
 
     def gelu(x):
         return jax.nn.gelu(x, approximate=True)
 
-    def hidden(m, g, o_a, o_b):
-        put(g, gelu(o_a), gelu(o_b))
-
-    def first_state(m, g, o_a, o_b):
-        s_a = (st_a[pl.ds(g, STRIDE)] + o_a).astype(BF).astype(F32)
-        s_b = (st_b[pl.ds(g, STRIDE)] + o_b).astype(BF).astype(F32)
-        st_a[pl.ds(g, STRIDE)] = s_a
-        st_b[pl.ds(g, STRIDE)] = s_b
-        put(g, *normed(s_a, s_b, gain_a, gain_b))
-
-    def second_state(m, g, o_a, o_b):
-        s_a, s_b = st_a[pl.ds(g, STRIDE)], st_b[pl.ds(g, STRIDE)]
+    def hidden(v, m, g, rows, o_a, o_b):
+        put(v, g, gelu(o_a), gelu(o_b), rows)
+
+    def first_state(v, m, g, rows, o_a, o_b):
+        s_a = (st_a[pl.ds(g, rows)] + o_a).astype(BF).astype(F32)
+        s_b = (st_b[pl.ds(g, rows)] + o_b).astype(BF).astype(F32)
+        st_a[pl.ds(g, rows)] = s_a
+        st_b[pl.ds(g, rows)] = s_b
+        put(v, g, *normed(s_a, s_b, gain_a, gain_b), rows)
+
+    def second_state(v, m, g, rows, o_a, o_b):
+        s_a, s_b = st_a[pl.ds(g, rows)], st_b[pl.ds(g, rows)]
         t_a = (s_a + o_a).astype(BF)
         t_b = (s_b + o_b).astype(BF)
-        r = pl.multiple_of(32 * m, 32)
-        fin[0, pl.ds(r, 32), 0:128] = t_a[16:48]
-        fin[0, pl.ds(r, 32), 128:256] = t_b[16:48]
-        y_a, y_b = oc_a[pl.ds(g, STRIDE)], oc_b[pl.ds(g, STRIDE)]
+        if rows == STRIDE:
+            r = pl.multiple_of(32 * m, 32)
+            fin[0, pl.ds(r, 32), 0:128] = t_a[16:48]
+            fin[0, pl.ds(r, 32), 128:256] = t_b[16:48]
+        y_a, y_b = oc_a[pl.ds(g, rows)], oc_b[pl.ds(g, rows)]
         mask = y_b[:, 96:97]
         put(
+            v,
             g,
             (y_a + 0.5 * (s_a + t_a.astype(F32))) * mask,
             (y_b + 0.5 * (s_b + t_b.astype(F32))) * mask,
-        )
-
-    def mixed(m, g, o_a, o_b):
+            rows,
+        )
+
+    def mixed(v, m, g, rows, o_a, o_b):
         n_a, n_b = normed(
             o_a.astype(BF).astype(F32), o_b.astype(BF).astype(F32), ocean_a, ocean_b
         )
@@ -357,67 +389,81 @@
         nrm[pl.ds(r, 32), 0:128] = n_a[16:48].astype(BF)
         nrm[pl.ds(r, 32), 128:256] = n_b[16:48].astype(BF)
 
-    convolve(20, 0, hidden)
-    replicate()
-    loads[4].wait()
-    pair[3].wait_recv()
-    prepare(1)
-    convolve(19, 1, first_state)
-    replicate()
-    convolve(18, 0, hidden)
-    replicate()
-    convolve(17, 1, second_state)
-    replicate()
-    loads[5].wait()
-    pair[4].wait_recv()
-    prepare(2)
-    convolve(16, 2, mixed)
-
-    loads[6].wait()
-    loads[7].wait()
-
-    @pl.loop(0, 2)
-    def _(m):
-        r = pl.multiple_of(256 * m, 256)
-        h = jnp.dot(nrm[pl.ds(r, 256), :][:, :160], miv[...], preferred_element_type=F32)
+    outs = []
+
+    def send_out(n, k, src, dst):
+        copy = pltpu.make_async_remote_copy(
+            src_ref=src,
+            dst_ref=dst,
+            send_sem=osem_s.at[k],
+            recv_sem=osem_r.at[k],
+            device_id=partner,
+            device_id_type=MESH,
+        )
+        copy.start()
+        outs.append(copy)
+
+    mine = pl.ds(pl.multiple_of(512 * c, 512), 512)
+
+    def stored(n, b):
+        return lax.dot_general(
+            fin[n, 256 * b : 256 * b + 256][:, :160], tsel[b], TN, preferred_element_type=F32
+        )
+
+    def atmosphere_out():
+        for b in range(2):
+            o = pl.multiple_of(256 * jnp.where(c == 0, b, 1 - b), 256)
+            t_a = stored(0, b).astype(BF)
+            for k in range(2):
+                obuf[0, k, :, pl.ds(o, 256)] = t_a[80 * k : 80 * k + 80]
+        send_out(0, 0, obuf.at[0, pc], out_a.at[:, mine])
+        out_a[:, mine] = obuf[0, c]
+
+    def ocean_out(b):
+        h = jnp.dot(
+            nrm[256 * b : 256 * b + 256, :][:, :160], miv[...], preferred_element_type=F32
+        )
         h = gelu(h).astype(BF)
         u = lax.dot_general(h, mov[...], NT, preferred_element_type=F32).astype(BF)
-        fin[1, pl.ds(r, 256), 0:160] = u
-
-    for b in range(2):
+        fin[1, 256 * b : 256 * b + 256, 0:160] = u
         q = pl.multiple_of(256 * jnp.where(c == 0, b, 3 - b), 256)
         o = pl.multiple_of(256 * jnp.where(c == 0, b, 1 - b), 256)
-        t_a = lax.dot_general(
-            fin[0, 256 * b : 256 * b + 256][:, :160], tsel[b], TN, preferred_element_type=F32
-        )
-        u = lax.dot_general(
-            fin[1, 256 * b : 256 * b + 256][:, :160], tsel[b], TN, preferred_element_type=F32
-        )
+        u = stored(1, b)
         w_row = wet[:, pl.ds(q, 256)].astype(F32)
         for k in range(2):
-            rows = slice(80 * k, 80 * k + 80)
-            obuf[0, k, :, pl.ds(o, 256)] = t_a[rows].astype(BF)
             obuf[1, k, :, pl.ds(o, 256)] = (
-                xo[k, :, pl.ds(q, 256)].astype(F32) + w_row * u[rows]
+                xo[k, :, pl.ds(q, 256)].astype(F32) + w_row * u[80 * k : 80 * k + 80]
             ).astype(BF)
-
-    mine = pl.ds(pl.multiple_of(512 * c, 512), 512)
-    outs = []
-    for n, ref in enumerate((out_a, out_o)):
-        outs.append(
-            pltpu.make_async_remote_copy(
-                src_ref=obuf.at[n, pc],
-                dst_ref=ref.at[:, mine],
-                send_sem=osem_s.at[n],
-                recv_sem=osem_r.at[n],
-                device_id=partner,
-                device_id_type=MESH,
-            )
-        )
-    for copy in outs:
-        copy.start()
-    out_a[:, mine] = obuf[0, c]
-    out_o[:, mine] = obuf[1, c]
+        here = pl.ds(pl.multiple_of(512 * c + o, 256), 256)
+        send_out(1, 1 + b, obuf.at[1, pc, :, pl.ds(o, 256)], out_o.at[:, here])
+        out_o[:, here] = obuf[1, c, :, pl.ds(o, 256)]
+
+    steps = []
+    for k, (n, wi, epilogue) in enumerate(
+        ((20, 0, hidden), (19, 1, first_state), (18, 0, hidden), (17, 1, second_state), (16, 2, mixed))
+    ):
+        for i, (lo, hi) in enumerate(bounds(n)):
+            steps.append((k, n, wi, epilogue, i, lo, hi))
+    ready = 0
+    for at, (k, n, wi, epilogue, i, lo, hi) in enumerate(steps):
+        while ready < min(at + AHEAD, len(steps)):
+            d = steps[ready]
+            if d[0] > k:
+                done = steps[at - 1] if at else None
+                need = min(d[6] + 2, d[1] + 1)
+                if d[0] > k + 1 or done is None or done[0] < k or done[6] < min(need, n):
+                    break
+            products(d[0] % 2, d[1], d[2], d[5], d[6])
+            ready += 1
+        finish(1 - k % 2, n, epilogue, lo, hi)
+        if i == 0 and k < 4:
+            replicate(1 - k % 2)
+        if k == 4 and i == 0:
+            atmosphere_out()
+        if k == 4 and hi >= 8 and lo < 8:
+            ocean_out(0)
+    ocean_out(1)
+
     for copy in halo_copies:
         copy.wait_send()
     for copy in pair:
@@ -426,21 +472,34 @@
         copy.wait()
 
 
+def write_out(a, o, out_a, out_o, sem):
+    copies = [
+        pltpu.make_async_copy(a, out_a, sem.at[0]),
+        pltpu.make_async_copy(o, out_o, sem.at[1]),
+    ]
+    for copy in copies:
+        copy.start()
+    for copy in copies:
+        copy.wait()
+
+
 def per_device(
     atm_state, ocean_state, wet_mask, neighbours, west_rim, east_rim, atm_gain,
     atm_conv_in, atm_conv_out, ocean_conv, ocean_gain, mlp_in, mlp_out,
 ):
     vmem = pl.BlockSpec(memory_space=pltpu.VMEM)
     anym = pl.BlockSpec(memory_space=pl.ANY)
+    hbm = pl.BlockSpec(memory_space=pltpu.HBM)
     pixels = atm_state.shape[1]
-    taps = [jnp.transpose(w, (1, 0, 2)) for w in (atm_conv_in, atm_conv_out, ocean_conv)]
+    pin = lambda x: pltpu.with_memory_space_constraint(x, pltpu.HBM)
+    taps = [pin(jnp.transpose(w, (1, 0, 2))) for w in (atm_conv_in, atm_conv_out, ocean_conv)]
     out = jax.ShapeDtypeStruct((CH, pixels), BF)
     dma = pltpu.SemaphoreType.DMA
-    return pl.pallas_call(
+    parts = pl.pallas_call(
         kernel,
         name="coupled_step",
         out_shape=(out, out),
-        in_specs=[anym] + [vmem] * 3 + [anym] * 7,
+        in_specs=[anym] * 11,
         out_specs=(vmem, vmem),
         scratch_shapes=[
             pltpu.VMEM((2, CH, pixels), BF),
@@ -457,35 +516,48 @@
             pltpu.VMEM((BUF, 128), F32),
             pltpu.VMEM((BUF, 128), F32),
             pltpu.VMEM((BUF, 128), F32),
-            pltpu.VMEM((BUF, 128), BF),
-            pltpu.VMEM((BC, 128), BF),
+            pltpu.VMEM((2, BUF, 128), BF),
+            pltpu.VMEM((2, BC, 128), BF),
             pltpu.VMEM((BUF, 512), F32),
             pltpu.VMEM((576, 256), BF),
             pltpu.VMEM((2, 576, 256), BF),
             pltpu.VMEM((2, 2, CH, 512), BF),
             pltpu.VMEM((8, pixels), jnp.int32),
-            dma((8,)),
+            pltpu.VMEM((1, pixels), jnp.int32),
+            pltpu.VMEM((1, C), F32),
+            pltpu.VMEM((1, C), F32),
+            pltpu.VMEM((368, 256), BF),
+            pltpu.VMEM((304, 256), BF),
+            dma((11,)),
             dma((5,)),
             dma((5,)),
             dma((4,)),
             dma((2, 2)),
-            dma((2,)),
-            dma((2,)),
+            dma((3,)),
+            dma((3,)),
         ],
         compiler_params=pltpu.CompilerParams(
-            collective_id=0, has_side_effects=True, vmem_limit_bytes=67_043_328
+            collective_id=0, has_side_effects=True, vmem_limit_bytes=48 * 1024 * 1024
         ),
     )(
-        neighbours,
-        wet_mask.reshape(1, pixels),
-        atm_gain.reshape(1, C),
-        ocean_gain.reshape(1, C),
-        atm_state,
-        ocean_state,
+        pin(neighbours),
+        pin(wet_mask.reshape(1, pixels)),
+        pin(atm_gain.reshape(1, C)),
+        pin(ocean_gain.reshape(1, C)),
+        pin(atm_state),
+        pin(ocean_state),
         *taps,
-        jnp.transpose(mlp_in),
-        mlp_out,
+        pin(jnp.transpose(mlp_in)),
+        pin(mlp_out),
     )
+    return pl.pallas_call(
+        write_out,
+        name="write_out",
+        out_shape=(out, out),
+        in_specs=[vmem] * 2,
+        out_specs=(hbm, hbm),
+        scratch_shapes=[dma((2,))],
+    )(*[pltpu.with_memory_space_constraint(x, pltpu.VMEM) for x in parts])
 
 
 def solution(mesh):

time: 33.9 us -> 28.7 us (0.85)
  Pallas kernels: 30.8 us -> 27.9 us
  local copies, waits for them, and re-layouts: 2.3 us -> 0 us
    pallas_call x1, Pallas kernels: 30.8 us -> 27.2 us  [per_device(): pl.pallas_call(kernel, name='coupled_step', out_shape=(out, out), in_spec...]
    unnamed x4 -> x0, local copies, waits for them, and re-layouts: 2.3 us -> none
    pallas_call x0 -> x1, Pallas kernels: none -> 0.74 us  [per_device(): pl.pallas_call(write_out, name='write_out', out_shape=(out, out), in_spec...]
where the time goes in v3:
time: 28.7 us; the launch traced here: 28.6 us
  Pallas kernels  27.9 us (97%)
  between operations  0.64 us (2%)
    pallas_call x1, Pallas kernels, per_device(): pl.pallas_call(kernel, name='coupled_step', out_shape=(out, out), in_spec...  27.2 us
    pallas_call x1, Pallas kernels, per_device(): pl.pallas_call(write_out, name='write_out', out_shape=(out, out), in_spec...  0.74 us

profile of v3, /device:TPU:1, one launch (start us, length us, event | category | flops | bytes accessed | tf_op | source)
XLA Modules:
  0.0 28.6 jit_solution(16967250365058163736)
XLA Ops:
  0.6 27.2 %coupled_step.1 = (bf16[80,1024]{1,0:T(8,128)(2,1)S(1)}, bf16[80,1024]{1,0:T(8,128)(2,1)S(1)}) custom-call(s32[8,1024]{1,0:T(8,128)} %nb.1, s32[1,1024]{1,0:T(1,128)} %bitcast.11, f32[1,160]{1,0:T(1,128)} %bitcast.12, f32[1,160]{1,0:T(1,128)} %bitcast.13, bf16[80,1024]{1,0:T(8,128)(2,1)} %atm.1, bf16[80,1024]{1,0:T(8,128)(2,1)} %oc.1, ...), custom_call_target="tpu_custom_call" | custom-call | tf_op jit(solution)/shard_map/coupled_step/pallas_call | solution.py:498
  27.8 0.7 %write_out.1 = (bf16[80,1024]{1,0:T(8,128)(2,1)}, bf16[80,1024]{1,0:T(8,128)(2,1)}) custom-call(bf16[80,1024]{1,0:T(8,128)(2,1)S(1)} %get-tuple-element.4.a, bf16[80,1024]{1,0:T(8,128)(2,1)S(1)} %get-tuple-element.5.o), custom_call_target="tpu_custom_call" | custom-call | tf_op jit(solution)/shard_map/write_out/pallas_call | solution.py:553

commit v4 on v3

--- a/solution.py
+++ b/solution.py
@@ -31,18 +31,14 @@
     return jnp.where(hit, 1.0, 0.0).astype(BF)
 
 
-def tap_slot(dyi, dxi):
-    m = 3 * dyi + dxi
-    return 0 if m == 4 else (m + 1 if m < 4 else m)
-
-
 def kernel(
     nb, wet_h, ga_h, go_h, atm, oc, w1, w2, w3, mi, mo,
     out_a, out_o,
-    xa, xo, wraw, wb, miv, mov, keys, tsel, sbuf, halo, st_a, st_b, oc_a, oc_b,
+    xa, xo, wraw_0, wraw_1, wraw_2, wb, miv, mov, keys, tsel, sbuf, halo, st_a, st_b, oc_a, oc_b,
     va, bc, pbuf, nrm, fin, obuf, nbv, wet, ga, go, hsel, osel,
     lsem, psem_s, psem_r, hsem_s, hsem_r, osem_s, osem_r,
 ):
+    wraw = (wraw_0, wraw_1, wraw_2)
     sectors = lax.axis_size("sector")
     s = lax.axis_index("sector")
     c = lax.axis_index("chan")
@@ -63,22 +59,32 @@
         pltpu.make_async_copy(nb, nbv, lsem.at[0]),
         pltpu.make_async_copy(atm, xa.at[c], lsem.at[1]),
         pltpu.make_async_copy(oc, xo.at[c], lsem.at[2]),
-        pltpu.make_async_copy(w1, wraw.at[0, c], lsem.at[3]),
-        pltpu.make_async_copy(w2, wraw.at[1, c], lsem.at[4]),
-        pltpu.make_async_copy(w3, wraw.at[2, c], lsem.at[5]),
+        pltpu.make_async_copy(w1, wraw[0].at[c], lsem.at[3]),
+        pltpu.make_async_copy(w2, wraw[1].at[c], lsem.at[4]),
+        pltpu.make_async_copy(w3, wraw[2].at[c], lsem.at[5]),
         pltpu.make_async_copy(mi, miv, lsem.at[6]),
         pltpu.make_async_copy(mo, mov, lsem.at[7]),
         pltpu.make_async_copy(wet_h, wet, lsem.at[8]),
         pltpu.make_async_copy(ga_h, ga, lsem.at[9]),
         pltpu.make_async_copy(go_h, go, lsem.at[10]),
     ]
-    for load in loads:
-        load.start()
+    for n in (0, 1, 2, 8):
+        loads[n].start()
     loads[0].wait()
 
+    v = nbv[:, 0:128]
+    lane = iota((8, 128), 1)
+    sample = lax.shift_right_logical(lane, 5) == 1
+    beyond = v >= 1024
+    cycle = jnp.where(beyond, v & 31, lax.shift_right_logical(v, 5))
+    side = jnp.where(beyond, jnp.where(v < 1056, 1, 2), 0)
+    code = jnp.max(jnp.where(sample, 4 * cycle + side, 0), axis=1, keepdims=True)
+    side = code & 3
+    towards = 3 * lax.shift_right_logical(code, 2) + jnp.where(side == 0, 1, 2 * side - 2)
+
     for b in range(8):
-        lane = iota((8, 128), 1)
-        v = jnp.broadcast_to(nbv[3:4, 128 * b : 128 * b + 128], (8, 128))
+        v = jnp.where(towards == 3, nbv[:, 128 * b : 128 * b + 128], 0)
+        v = jnp.broadcast_to(jnp.max(v, axis=0, keepdims=True), (8, 128))
         inside = v < 1024
         hop = jnp.where(inside, v - 128 * b, lane)
         col = jnp.where(inside, 1, 0)
@@ -105,6 +111,18 @@
         (hh >= 105) & (hh < 122), 32 * (hh - 105) + jnp.where(far, 31, 0), -1
     )
     z16 = jnp.zeros((16, 256), BF)
+
+    def picked(keys_h, key_q, lo, hi):
+        parts = []
+        for d in (0, 128):
+            rows = slice(d + lo, d + hi)
+            if lo:
+                parts.append(jnp.zeros((lo, 256), BF))
+            parts.append(onehot(keys_h[rows] == key_q))
+            if hi < 128:
+                parts.append(jnp.zeros((128 - hi, 256), BF))
+        return jnp.concatenate(parts, axis=0)
+
     for t in range(2):
         total = jnp.zeros((96, 256), F32)
         for b in range(3):
@@ -113,10 +131,10 @@
             x_a = jnp.concatenate([xa[c, :, q : q + 256], z16], axis=0)
             x_o = jnp.concatenate([xo[c, :, q : q + 256], wet16[:, q : q + 256]], axis=0)
             total = total + lax.dot_general(
-                x_a, onehot(key_a == key_q), NT, preferred_element_type=F32
+                x_a, picked(key_a, key_q, *((0, 48), (32, 80), (80, 112))[b]), NT, preferred_element_type=F32
             )
             total = total + lax.dot_general(
-                x_o, onehot(key_o == key_q), NT, preferred_element_type=F32
+                x_o, picked(key_o, key_q, 96, 128), NT, preferred_element_type=F32
             )
         sbuf[t, 0] = total[:, :128].astype(BF)
         sbuf[t, 1] = total[:, 128:].astype(BF)
@@ -152,27 +170,34 @@
     window = pl.ds(pl.multiple_of(256 * pc, 256), 768)
     pair = [
         to_partner(atm.at[:, window], xa.at[c, :, window], 0),
-        to_partner(w1, wraw.at[0, c], 1),
+        to_partner(w1, wraw[0].at[c], 1),
         to_partner(oc.at[:, window], xo.at[c, :, window], 2),
-        to_partner(w2, wraw.at[1, c], 3),
-        to_partner(w3, wraw.at[2, c], 4),
+        to_partner(w2, wraw[1].at[c], 3),
+        to_partner(w3, wraw[2].at[c], 4),
     ]
     for copy in pair:
         copy.start()
+    for n in (3, 9, 10, 4, 5, 6, 7):
+        loads[n].start()
 
     for b in range(3):
         q = pl.multiple_of(256 * jnp.where(c == 0, b, 3 - b), 256)
         key_q = keys[c, 0:1, pl.ds(q, 256)] - 256 * b
         tsel[b] = onehot(iota((256, 256), 0) == key_q)
+
+    slots = [
+        jnp.max(jnp.where(towards == m, iota((8, 1), 0) + 1, 0)) if m != 4 else 0
+        for m in range(9)
+    ]
 
     def prepare(n):
         wb[n, :, 480:512] = jnp.zeros((512, 32), BF)
         wb[n, 480:512, :] = jnp.zeros((32, 512), BF)
         for dyi in range(3):
             for dxi in range(3):
-                k = jnp.where(c == 0, tap_slot(dyi, dxi), tap_slot(2 - dyi, dxi))
-                w_0 = wraw[n, 0, k]
-                w_1 = wraw[n, 1, k]
+                k = jnp.where(c == 0, slots[3 * dyi + dxi], slots[3 * (2 - dyi) + dxi])
+                w_0 = wraw[n][0, k]
+                w_1 = wraw[n][1, k]
                 for lanes, dst, width in (
                     (slice(0, 128), 128 * dyi, 128),
                     (slice(128, 160), 384 + 32 * dyi, 32),
@@ -281,16 +306,18 @@
         [halo[0, 0:80], halo[1, 0:80]] + [h_1] * 2 + [halo[0, 80:96]] * 2, axis=0
     )
     v_a = lax.dot_general(hsel[...], h_atm, NT, preferred_element_type=F32)
-    v_o = lax.dot_general(osel[...], h_oc, NT, preferred_element_type=F32)
     for k in range(23):
         rows = slice(16 * k, 16 * k + 16)
         g = STRIDE * k
         st_a[g : g + 16] = v_a[rows, :128]
         st_b[g : g + 16] = v_a[rows, 128:]
         put(0, g, *normed(v_a[rows, :128], v_a[rows, 128:], gain_a, gain_b), rows=16)
-        if k < 19:
-            oc_a[g : g + 16] = v_o[rows, :128]
-            oc_b[g : g + 16] = v_o[rows, 128:]
+    v_o = lax.dot_general(osel[...], h_oc, NT, preferred_element_type=F32)
+    for k in range(19):
+        rows = slice(16 * k, 16 * k + 16)
+        g = STRIDE * k
+        oc_a[g : g + 16] = v_o[rows, :128]
+        oc_b[g : g + 16] = v_o[rows, 128:]
 
     group = lax.shift_right_logical(iota((1, 128), 1), 5)
 
@@ -327,7 +354,10 @@
 
         @pl.loop(lo, hi, unroll=True)
         def _(m):
-            piece(m, pl.multiple_of(STRIDE * m + STRIDE, STRIDE), STRIDE)
+            if n > 16:
+                piece(m, pl.multiple_of(STRIDE * m + STRIDE, STRIDE), STRIDE)
+            else:
+                piece(m, pl.multiple_of(STRIDE * m + STRIDE + 16, 16), 32)
 
         if hi == n and n > 16:
             piece(n, STRIDE * n + STRIDE, 16)
@@ -351,7 +381,8 @@
             ref[v, at + 48 : at + 64, lanes] = mix(own, nxt)
 
     def gelu(x):
-        return jax.nn.gelu(x, approximate=True)
+        half = 0.5 * x
+        return half + half * jnp.tanh(x * (0.7978845608028654 + 0.035677408136300125 * (x * x)))
 
     def hidden(v, m, g, rows, o_a, o_b):
         put(v, g, gelu(o_a), gelu(o_b), rows)
@@ -386,8 +417,8 @@
             o_a.astype(BF).astype(F32), o_b.astype(BF).astype(F32), ocean_a, ocean_b
         )
         r = pl.multiple_of(32 * m, 32)
-        nrm[pl.ds(r, 32), 0:128] = n_a[16:48].astype(BF)
-        nrm[pl.ds(r, 32), 128:256] = n_b[16:48].astype(BF)
+        nrm[pl.ds(r, 32), 0:128] = n_a.astype(BF)
+        nrm[pl.ds(r, 32), 128:256] = n_b.astype(BF)
 
     outs = []
 
@@ -424,11 +455,10 @@
             nrm[256 * b : 256 * b + 256, :][:, :160], miv[...], preferred_element_type=F32
         )
         h = gelu(h).astype(BF)
-        u = lax.dot_general(h, mov[...], NT, preferred_element_type=F32).astype(BF)
-        fin[1, 256 * b : 256 * b + 256, 0:160] = u
+        u = lax.dot_general(mov[...], h, NT, preferred_element_type=F32).astype(BF)
         q = pl.multiple_of(256 * jnp.where(c == 0, b, 3 - b), 256)
         o = pl.multiple_of(256 * jnp.where(c == 0, b, 1 - b), 256)
-        u = stored(1, b)
+        u = jnp.dot(u, tsel[b], preferred_element_type=F32)
         w_row = wet[:, pl.ds(q, 256)].astype(F32)
         for k in range(2):
             obuf[1, k, :, pl.ds(o, 256)] = (
@@ -504,7 +534,9 @@
         scratch_shapes=[
             pltpu.VMEM((2, CH, pixels), BF),
             pltpu.VMEM((2, CH, pixels), BF),
-            pltpu.VMEM((3, 2, 9, CH, C), BF),
+            pltpu.VMEM((2, 9, CH, C), BF),
+            pltpu.VMEM((2, 9, CH, C), BF),
+            pltpu.VMEM((2, 9, CH, C), BF),
             pltpu.VMEM((3, 512, 512), BF),
             pltpu.VMEM((C, 640), BF),
             pltpu.VMEM((C, 640), BF),

time: 28.7 us -> 28.6 us (level)
  no operation moved by 1% of the time
where the time goes in v4:
time: 28.6 us; the launch traced here: 28.5 us
  Pallas kernels  27.9 us (98%)
  between operations  0.64 us (2%)
    pallas_call x1, Pallas kernels, per_device(): pl.pallas_call(kernel, name='coupled_step', out_shape=(out, out), in_spec...  27.1 us
    pallas_call x1, Pallas kernels, per_device(): pl.pallas_call(write_out, name='write_out', out_shape=(out, out), in_spec...  0.74 us

profile of v4, /device:TPU:1, one launch (start us, length us, event | category | flops | bytes accessed | tf_op | source)
XLA Modules:
  0.0 28.5 jit_solution(6637667960258693024)
XLA Ops:
  0.6 27.1 %coupled_step.1 = (bf16[80,1024]{1,0:T(8,128)(2,1)S(1)}, bf16[80,1024]{1,0:T(8,128)(2,1)S(1)}) custom-call(s32[8,1024]{1,0:T(8,128)} %nb.1, s32[1,1024]{1,0:T(1,128)} %bitcast.11, f32[1,160]{1,0:T(1,128)} %bitcast.12, f32[1,160]{1,0:T(1,128)} %bitcast.13, bf16[80,1024]{1,0:T(8,128)(2,1)} %atm.1, bf16[80,1024]{1,0:T(8,128)(2,1)} %oc.1, ...), custom_call_target="tpu_custom_call" | custom-call | tf_op jit(solution)/shard_map/coupled_step/pallas_call | solution.py:528
  27.8 0.7 %write_out.1 = (bf16[80,1024]{1,0:T(8,128)(2,1)}, bf16[80,1024]{1,0:T(8,128)(2,1)}) custom-call(bf16[80,1024]{1,0:T(8,128)(2,1)S(1)} %get-tuple-element.4.a, bf16[80,1024]{1,0:T(8,128)(2,1)S(1)} %get-tuple-element.5.o), custom_call_target="tpu_custom_call" | custom-call | tf_op jit(solution)/shard_map/write_out/pallas_call | solution.py:585

commit v5 on v4

--- a/solution.py
+++ b/solution.py
@@ -455,18 +455,21 @@
             nrm[256 * b : 256 * b + 256, :][:, :160], miv[...], preferred_element_type=F32
         )
         h = gelu(h).astype(BF)
-        u = lax.dot_general(mov[...], h, NT, preferred_element_type=F32).astype(BF)
         q = pl.multiple_of(256 * jnp.where(c == 0, b, 3 - b), 256)
         o = pl.multiple_of(256 * jnp.where(c == 0, b, 1 - b), 256)
-        u = jnp.dot(u, tsel[b], preferred_element_type=F32)
         w_row = wet[:, pl.ds(q, 256)].astype(F32)
-        for k in range(2):
-            obuf[1, k, :, pl.ds(o, 256)] = (
-                xo[k, :, pl.ds(q, 256)].astype(F32) + w_row * u[80 * k : 80 * k + 80]
-            ).astype(BF)
         here = pl.ds(pl.multiple_of(512 * c + o, 256), 256)
+
+        def channels(k):
+            u = lax.dot_general(
+                mov[pl.ds(pl.multiple_of(CH * k, 16), CH)], h, NT, preferred_element_type=F32
+            )
+            u = jnp.dot(u.astype(BF), tsel[b], preferred_element_type=F32)
+            return (xo[k, :, pl.ds(q, 256)].astype(F32) + w_row * u).astype(BF)
+
+        obuf[1, pc, :, pl.ds(o, 256)] = channels(pc)
         send_out(1, 1 + b, obuf.at[1, pc, :, pl.ds(o, 256)], out_o.at[:, here])
-        out_o[:, here] = obuf[1, c, :, pl.ds(o, 256)]
+        out_o[:, here] = channels(c)
 
     steps = []
     for k, (n, wi, epilogue) in enumerate(
@@ -503,10 +506,13 @@
 
 
 def write_out(a, o, out_a, out_o, sem):
-    copies = [
-        pltpu.make_async_copy(a, out_a, sem.at[0]),
-        pltpu.make_async_copy(o, out_o, sem.at[1]),
-    ]
+    copies = []
+    for n, (src, dst) in enumerate(((a, out_a), (o, out_o))):
+        for k in range(4):
+            lanes = pl.ds(256 * k, 256)
+            copies.append(
+                pltpu.make_async_copy(src.at[:, lanes], dst.at[:, lanes], sem.at[4 * n + k])
+            )
     for copy in copies:
         copy.start()
     for copy in copies:
@@ -588,7 +594,7 @@
         out_shape=(out, out),
         in_specs=[vmem] * 2,
         out_specs=(hbm, hbm),
-        scratch_shapes=[dma((2,))],
+        scratch_shapes=[dma((8,))],
     )(*[pltpu.with_memory_space_constraint(x, pltpu.VMEM) for x in parts])
 
 

time: 28.6 us -> 28.6 us (level)
  no operation moved by 1% of the time
where the time goes in v5:
time: 28.6 us; the launch traced here: 28.5 us
  Pallas kernels  27.8 us (97%)
  between operations  0.64 us (2%)
    pallas_call x1, Pallas kernels, per_device(): pl.pallas_call(kernel, name='coupled_step', out_shape=(out, out), in_spec...  27 us
    pallas_call x1, Pallas kernels, per_device(): pl.pallas_call(write_out, name='write_out', out_shape=(out, out), in_spec...  0.78 us

profile of v5, /device:TPU:1, one launch (start us, length us, event | category | flops | bytes accessed | tf_op | source)
XLA Modules:
  0.0 28.5 jit_solution(9704977262656411491)
XLA Ops:
  0.6 27.0 %coupled_step.1 = (bf16[80,1024]{1,0:T(8,128)(2,1)S(1)}, bf16[80,1024]{1,0:T(8,128)(2,1)S(1)}) custom-call(s32[8,1024]{1,0:T(8,128)} %nb.1, s32[1,1024]{1,0:T(1,128)} %bitcast.11, f32[1,160]{1,0:T(1,128)} %bitcast.12, f32[1,160]{1,0:T(1,128)} %bitcast.13, bf16[80,1024]{1,0:T(8,128)(2,1)} %atm.1, bf16[80,1024]{1,0:T(8,128)(2,1)} %oc.1, ...), custom_call_target="tpu_custom_call" | custom-call | tf_op jit(solution)/shard_map/coupled_step/pallas_call | solution.py:534
  27.7 0.8 %write_out.1 = (bf16[80,1024]{1,0:T(8,128)(2,1)}, bf16[80,1024]{1,0:T(8,128)(2,1)}) custom-call(bf16[80,1024]{1,0:T(8,128)(2,1)S(1)} %get-tuple-element.4.a, bf16[80,1024]{1,0:T(8,128)(2,1)S(1)} %get-tuple-element.5.o), custom_call_target="tpu_custom_call" | custom-call | tf_op jit(solution)/shard_map/write_out/pallas_call | solution.py:591

commit v6 on v5

--- a/solution.py
+++ b/solution.py
@@ -302,9 +302,6 @@
             ).wait_recv()
     h_1 = halo[1, 48:80]
     h_atm = jnp.concatenate([halo[0, 0:80], halo[1, 0:80]] + [h_1] * 3, axis=0)
-    h_oc = jnp.concatenate(
-        [halo[0, 0:80], halo[1, 0:80]] + [h_1] * 2 + [halo[0, 80:96]] * 2, axis=0
-    )
     v_a = lax.dot_general(hsel[...], h_atm, NT, preferred_element_type=F32)
     for k in range(23):
         rows = slice(16 * k, 16 * k + 16)
@@ -312,12 +309,16 @@
         st_a[g : g + 16] = v_a[rows, :128]
         st_b[g : g + 16] = v_a[rows, 128:]
         put(0, g, *normed(v_a[rows, :128], v_a[rows, 128:], gain_a, gain_b), rows=16)
-    v_o = lax.dot_general(osel[...], h_oc, NT, preferred_element_type=F32)
-    for k in range(19):
-        rows = slice(16 * k, 16 * k + 16)
-        g = STRIDE * k
-        oc_a[g : g + 16] = v_o[rows, :128]
-        oc_b[g : g + 16] = v_o[rows, 128:]
+    def ocean_halos():
+        h_oc = jnp.concatenate(
+            [halo[0, 0:80], halo[1, 0:80]] + [h_1] * 2 + [halo[0, 80:96]] * 2, axis=0
+        )
+        v_o = lax.dot_general(osel[...], h_oc, NT, preferred_element_type=F32)
+        for k in range(19):
+            rows = slice(16 * k, 16 * k + 16)
+            g = STRIDE * k
+            oc_a[g : g + 16] = v_o[rows, :128]
+            oc_b[g : g + 16] = v_o[rows, 128:]
 
     group = lax.shift_right_logical(iota((1, 128), 1), 5)
 
@@ -489,6 +490,8 @@
             products(d[0] % 2, d[1], d[2], d[5], d[6])
             ready += 1
         finish(1 - k % 2, n, epilogue, lo, hi)
+        if at == 0:
+            ocean_halos()
         if i == 0 and k < 4:
             replicate(1 - k % 2)
         if k == 4 and i == 0:

time: 28.6 us -> 28.6 us (level)
  no operation moved by 1% of the time
where the time goes in v6:
time: 28.6 us; the launch traced here: 28.4 us
  Pallas kernels  27.8 us (97%)
  between operations  0.64 us (2%)
    pallas_call x1, Pallas kernels, per_device(): pl.pallas_call(kernel, name='coupled_step', out_shape=(out, out), in_spec...  27 us
    pallas_call x1, Pallas kernels, per_device(): pl.pallas_call(write_out, name='write_out', out_shape=(out, out), in_spec...  0.78 us

profile of v6, /device:TPU:1, one launch (start us, length us, event | category | flops | bytes accessed | tf_op | source)
XLA Modules:
  0.0 28.4 jit_solution(7001021932135075862)
XLA Ops:
  0.6 27.0 %coupled_step.1 = (bf16[80,1024]{1,0:T(8,128)(2,1)S(1)}, bf16[80,1024]{1,0:T(8,128)(2,1)S(1)}) custom-call(s32[8,1024]{1,0:T(8,128)} %nb.1, s32[1,1024]{1,0:T(1,128)} %bitcast.11, f32[1,160]{1,0:T(1,128)} %bitcast.12, f32[1,160]{1,0:T(1,128)} %bitcast.13, bf16[80,1024]{1,0:T(8,128)(2,1)} %atm.1, bf16[80,1024]{1,0:T(8,128)(2,1)} %oc.1, ...), custom_call_target="tpu_custom_call" | custom-call | tf_op jit(solution)/shard_map/coupled_step/pallas_call | solution.py:537
  27.7 0.8 %write_out.1 = (bf16[80,1024]{1,0:T(8,128)(2,1)}, bf16[80,1024]{1,0:T(8,128)(2,1)}) custom-call(bf16[80,1024]{1,0:T(8,128)(2,1)S(1)} %get-tuple-element.4.a, bf16[80,1024]{1,0:T(8,128)(2,1)S(1)} %get-tuple-element.5.o), custom_call_target="tpu_custom_call" | custom-call | tf_op jit(solution)/shard_map/write_out/pallas_call | solution.py:594
